TPU v7x, 256 devices: a whole 4x4x8 slice. The times are simulated.
256 devices in a mesh: clip: 128 (over y_hi, x, z, core), strip: 2 (over y_lo).
Axes of the slice: x: 4, y: 4 (y_hi: 2, y_lo: 2; y = y_hi * 2 + y_lo), z: 8, core: 2. Of those that a mesh axis runs over, the one named last changes fastest.
Arguments:
- video: bfloat16 [256, 2, 32, 32, 256], P('clip', None, 'strip')
- gain_first: float32 [256], replicated, may hold values from 0.1 to 1.9
- conv_weight: bfloat16 [3, 3, 3, 256, 256], replicated, may hold values from -0.078125 to 0.078125
- gain_second: float32 [256], replicated, may hold values from 0.1 to 1.9
- proj_weight: bfloat16 [256, 256], replicated, may hold values from -0.375 to 0.375
- codes: int32 [256, 2, 32, 32], P('clip', None, 'strip'), may hold values from 0 to 1023
- ema_sum: float32 [1024, 256], replicated, may hold values from -12 to 12
- ema_count: float32 [1024], replicated, may hold values from 0.5 to 8
Outputs:
- latent: float32 [256, 2, 32, 32, 256], P('clip', None, 'strip')
- codebook: float32 [1024, 256], replicated
- code_count: float32 [1024], replicated
- clip_error: float32 [256], P('clip')
All inputs are finite; a program needn't handle non-finite values.
Results may differ from a plain program's by a relative error of at most 0.0029.
Values may be sent and summed in bfloat16 or wider, within the bound.
A program may use at most 64 MiB of HBM per device.

v0:
```python
import jax
import jax.numpy as jnp
from jax import lax
from jax.sharding import PartitionSpec as P

EMB = 256
CODES = 1024
GROUPS = 32


norm_eps = 1e-06
smooth_eps = 1e-05
ema_decay = 0.9


def copy_for_each(x, axis):
    peers = lax.axis_size(axis)
    return lax.all_to_all(jnp.broadcast_to(x[None], (peers, *x.shape)), axis, 0, 0, tiled=True)


def of_everyone(x, axis):
    return copy_for_each(x, axis).sum(axis=0)


def together(arrays, axis):
    ends = [0]
    for a in arrays:
        ends.append(ends[-1] + a.size)
    so_far = of_everyone(jnp.concatenate([a.ravel() for a in arrays]), axis)
    return tuple((so_far[b:e].reshape(a.shape) for a, b, e in zip(arrays, ends, ends[1:])))


def extended(cells, sides, width):
    for axis, dim in sides:
        count = lax.axis_size(axis)
        ends = count - 1
        head = lax.slice_in_dim(cells, 0, width, axis=dim)
        tail = lax.slice_in_dim(cells, cells.shape[dim] - width, cells.shape[dim], axis=dim)
        cells = jnp.concatenate(
            [
                lax.ppermute(tail, axis, [(i, (i + 1) % count) for i in range(ends)]),
                cells,
                lax.ppermute(head, axis, [((i + 1) % count, i) for i in range(ends)]),
            ],
            axis=dim,
        )
    return cells


def group_norm(values, gain_vec):
    shaped = values.reshape(values.shape[:4] + (GROUPS, values.shape[4] // GROUPS))
    members = (
        shaped.shape[1]
        * shaped.shape[2]
        * lax.axis_size("strip")
        * shaped.shape[3]
        * shaped.shape[5]
    )
    first_sum = jnp.sum(shaped, axis=(1, 2, 3, 5))
    second_sum = jnp.sum(shaped * shaped, axis=(1, 2, 3, 5))
    first_sum, second_sum = together((first_sum, second_sum), "strip")
    centre = first_sum / members
    spread = second_sum / members - centre * centre
    centre = centre[:, None, None, None, :, None]
    spread = spread[:, None, None, None, :, None]
    normed = (shaped - centre) * lax.rsqrt(spread + norm_eps)
    return normed.reshape(values.shape) * gain_vec


def smoothed_book(sums, counts, grand):
    smooth = (counts + smooth_eps) / (grand + CODES * smooth_eps) * grand
    return sums / smooth[:, None]


def body(video, gain_first, conv_weight, gain_second, proj_weight, codes, ema_sum, ema_count):
    batch_clips, frame_count, row_count, col_count, channels = video.shape
    values = video.astype(jnp.float32)
    act_first = jax.nn.silu(group_norm(values, gain_first)).astype(jnp.bfloat16)
    padded = extended(act_first, (("strip", 2),), 1)
    convolved = lax.conv_general_dilated(
        padded,
        conv_weight,
        (1, 1, 1),
        [(2, 0), (0, 0), (1, 1)],
        dimension_numbers=("NDHWC", "DHWIO", "NDHWC"),
        preferred_element_type=jnp.float32,
    )
    hidden = values + convolved
    act_second = jax.nn.silu(group_norm(hidden, gain_second)).astype(jnp.bfloat16)
    flat_latent = jnp.dot(
        act_second.reshape(-1, channels), proj_weight, preferred_element_type=jnp.float32
    )
    flat_codes = codes.reshape(-1)
    old_book = smoothed_book(ema_sum, ema_count, jnp.sum(ema_count))
    quantized = jnp.take(old_book, flat_codes, axis=0)
    squared = jnp.sum((flat_latent - quantized) ** 2, axis=1).reshape(batch_clips, -1)
    clip_tokens = squared.shape[1] * lax.axis_size("strip")
    error_sum = lax.psum(jnp.sum(squared, axis=1), "strip")
    clip_error = error_sum / (clip_tokens * EMB)
    code_sums = jax.ops.segment_sum(flat_latent, flat_codes, CODES)
    token_counts = jax.ops.segment_sum(jnp.ones(flat_codes.shape, jnp.float32), flat_codes, CODES)
    all_tokens = flat_codes.shape[0] * lax.axis_size("clip") * lax.axis_size("strip")
    grand_total = ema_decay * jnp.sum(ema_count) + (1.0 - ema_decay) * all_tokens
    total_sums, total_counts = lax.psum((code_sums, token_counts), ("clip", "strip"))
    code_count = ema_decay * ema_count + (1.0 - ema_decay) * total_counts
    codebook = smoothed_book(
        ema_decay * ema_sum + (1.0 - ema_decay) * total_sums, code_count, grand_total
    )
    latent = flat_latent.reshape(batch_clips, frame_count, row_count, col_count, EMB)
    return (latent, codebook, code_count, clip_error)


def solution(mesh):
    in_specs = (
        P("clip", None, "strip", None, None),
        P(),
        P(),
        P(),
        P(),
        P("clip", None, "strip", None),
        P(),
        P(),
    )
    out_specs = (P("clip", None, "strip", None, None), P(), P(), P("clip"))
    return jax.shard_map(body, mesh=mesh, in_specs=in_specs, out_specs=out_specs, check_vma=False)
```

profile of v0, /device:TPU:1, one launch (start us, length us, event | category | flops | bytes accessed | tf_op | source)
XLA Modules:
  0.0 388.8 jit_solution(11286395659139007540)
XLA Ops:
  7.2 1.9 convert_reduce_fusion
  12.5 5.8 %all_to_all.12 = f32[2,1,128]{2,1,0:T(1,128)S(1)} all-to-all(f32[2,1,128]{2,1,0:T(1,128)S(1)} %broadcast_in_dim.17), channel_id=1, replica_groups=mesh['clip'=128,'strip'=2] {'strip'}, dimensions={0} | all-to-all | bytes 2048 | tf_op jit(solution)/shard_map/all_to_all | solution.py:18
  21.6 2.2 fusion.8
  25.7 2.6 collective-permute-start
  30.4 3.9 collective-permute-done.1
  34.3 2.3 maximum_bitcast_fusion
  39.4 2.1 fusion.9
  41.5 10.3 %fusion.13 = f32[2,16,16,5,256]{4,2,3,1,0:T(8,128)S(1)} fusion(bf16[3,3,3,256,256]{4,3,2,1,0:T(8,128)(2,1)S(1)} %copy-done, bf16[2,18,2,8,7,256]{5,2,4,3,1,0:T(2,128)(2,1)S(1)} %fusion.9, pred[16,5]{0,1:T(8,128)(4,1)S(1)} %copy-done.4), kind=kOutput, calls=%fused_computation.25 | convolution fusion | flops 4530503680 | bytes 8224848 | tf_op jit(solution)/shard_map/conv_general_dilated | solution.py:80
  51.9 1.5 copy.32
  53.4 1.5 copy-done.1
  60.9 3.7 all-to-all-start.1
  65.6 1.7 all-to-all-done.1
  75.0 1.4 sub.49
  79.2 2.9 multiply_convert_fusion
  83.1 1.8 fusion.22
  84.8 13.0 %scatter_custom_fusion = f32[1024,256]{1,0:T(8,128)} fusion(s32[2048]{0:T(1024)S(1)} %reshape.208, f32[2048,256]{1,0:T(8,128)} %fusion.22, f32[]{:T(128)} %constant.15.clone.1), kind=kCustom, calls=%fused_computation.29 | custom fusion | flops 524288 | bytes 1049088 | tf_op jit(solution)/shard_map/scatter-add | solution.py:100
  101.6 15.4 %scatter_custom_fusion.1 = f32[1024]{0:T(1024)} fusion(s32[2048]{0:T(1024)S(1)} %reshape.208, f32[2048]{0:T(1024)} %broadcast.105, f32[]{:T(128)} %constant.15.clone.1), kind=kCustom, calls=%fused_computation.39 | custom fusion | flops 2048 | bytes 4608 | tf_op jit(solution)/shard_map/scatter-add | solution.py:101
  117.0 82.7 %psum.22 = f32[1024]{0:T(1024)} all-reduce(f32[1024]{0:T(1024)} %scatter_custom_fusion.1), channel_id=1, replica_groups=mesh['clip'=128,'strip'=2] {'clip','strip'}, use_global_device_ids=true, to_apply=%region_13.14 | all-reduce | flops 1024 | bytes 8192 | tf_op jit(solution)/shard_map/psum | solution.py:104
  199.7 1.9 divide_multiply_fusion.1
  201.7 160.3 %all-reduce.2.cloned.1.call-done = f32[1024,256]{1,0:T(8,128)} async-done(((f32[1024,256]{1,0:T(8,128)}), f32[1024,256]{1,0:T(8,128)}) %all-reduce.2.cloned.1.call-update) | async-done | bytes 1048592 | tf_op jit(solution)/shard_map/psum | solution.py:104
  362.0 3.2 broadcast_divide_fusion
  365.2 9.8 %gather_fusion = f32[2048,256]{1,0:T(8,128)} fusion(f32[1024,256]{1,0:T(8,128)} %get-tuple-element.10, s32[2048]{0:T(1024)S(1)} %broadcast_clamp_fusion), kind=kCustom, calls=%fused_computation | custom fusion | bytes 4202496 | tf_op jit(solution)/shard_map/jit(_take)/gather | solution.py:95
  375.0 2.5 multiply_reduce_fusion
  377.6 3.8 psum.23
  (66 shorter events, 34.9 us)
Async XLA Ops:
  7.2 34.3 %copy-start = (bf16[3,3,3,256,256]{4,3,2,1,0:T(8,128)(2,1)S(1)}, bf16[3,3,3,256,256]{4,3,2,1,0:T(8,128)(2,1)}, u32[]{:S(2)}) copy-start(bf16[3,3,3,256,256]{4,3,2,1,0:T(8,128)(2,1)} %param.10) | copy-start | bytes 10616836
  23.8 1.0 copy-start.3
  25.7 4.7 %collective-permute-start = (bf16[2,2,1,32,256]{4,2,3,0,1:T(2,128)(2,1)}, bf16[2,2,1,32,256]{4,2,3,0,1:T(2,128)(2,1)}, u32[]{:S(2)}, u32[]{:S(2)}) collective-permute-start(bf16[2,2,1,32,256]{4,2,3,0,1:T(2,128)(2,1)} %get-tuple-element.12), channel_id=1, source_target_pairs={{0,1},{2,3},{4,5},{6,7},{8,9},{10,11},{12,13},{14,15},{16,17},{18,... | collective-permute-start | bytes 196616 | tf_op jit(solution)/shard_map/ppermute | solution.py:41
  28.3 6.0 %collective-permute-start.1 = (bf16[2,2,1,32,256]{4,2,3,0,1:T(2,128)(2,1)}, bf16[2,2,1,32,256]{4,2,3,0,1:T(2,128)(2,1)}, u32[]{:S(2)}, u32[]{:S(2)}) collective-permute-start(bf16[2,2,1,32,256]{4,2,3,0,1:T(2,128)(2,1)} %get-tuple-element.13), channel_id=1, source_target_pairs={{1,0},{3,2},{5,4},{7,6},{9,8},{11,10},{13,12},{15,14},{17,16},{19,... | collective-permute-start | bytes 196616 | tf_op jit(solution)/shard_map/ppermute | solution.py:43
  39.4 2.1 copy-start.4
  51.9 3.0 copy-start.2
  53.4 1.5 copy-start.1
  60.9 6.4 %all-to-all-start.1 = ((f32[2,1,128]{2,1,0:T(1,128)}), f32[2,1,128]{2,1,0:T(1,128)}, u32[]{:S(2)}, u32[]{:S(2)}) async-start(f32[2,1,128]{2,1,0:T(1,128)} %broadcast_in_dim.18), calls=%async_computation.1 | async-start | bytes 2048 | tf_op jit(solution)/shard_map/all_to_all | solution.py:18
  64.7 297.3 %all-reduce.2.cloned.1.call-start = ((), (), s32[]{:S(2)}) async-start(), calls=%async_computation.2 | async-start | bytes 2097152 | tf_op jit(solution)/shard_map/psum | solution.py:104
  82.2 0.9 copy-start.5
  365.2 9.8 %copy-start.6 = (pred[2048]{0:T(1024)(128)(4,1)S(1)}, pred[2048]{0:T(1024)(128)(4,1)}, u32[]{:S(2)}) copy-start(pred[2048]{0:T(1024)(128)(4,1)} %compare_and_fusion) | copy-start | bytes 6148
Sparse Core Ops, SparseCore 0:
  97.9 263.9 all-reduce.1
where the time goes:
time: 392 us; the launch traced here: 389 us
  waiting for transfers between devices  166 us (42%)
  blocking collectives  92.3 us (24%)
  other arithmetic  59.1 us (15%)
  local copies, waits for them, and re-layouts  36.3 us (9%)
  between operations  15.5 us (4%)
  matrix products  12.1 us (3%)
  starting transfers between devices  7.6 us (2%)
    psum x1, waiting for transfers between devices, body(): lax.psum((code_sums, token_counts), ('clip', 'strip'))  160 us
    psum x1, blocking collectives, body(): lax.psum((code_sums, token_counts), ('clip', 'strip'))  82.7 us
    scatter-add x1, other arithmetic, body(): jax.ops.segment_sum(jnp.ones(flat_codes.shape, jnp.float32), flat_codes,...  15.4 us
    scatter-add x1, other arithmetic, body(): code_sums = jax.ops.segment_sum(flat_latent, flat_codes, CODES)  13 us
    conv_general_dilated x1, matrix products, body(): lax.conv_general_dilated(padded, conv_weight, (1, 1, 1), [(2, 0), (0, 0),...  10.3 us
    gather x1, local copies, waits for them, and re-layouts, body(): quantized = jnp.take(old_book, flat_codes, axis=0)  9.78 us
  transfers between devices with their start and end apart: 4, of which 3 were waited for; matrix products, arithmetic and copies ran while one was open for 6% of the time, Pallas kernels for 0%

commit v1 on v0

v1 whole, which is shorter than its diff:
```python
import functools

import jax
import jax.numpy as jnp
from jax import lax
from jax.experimental import pallas as pl
from jax.experimental.pallas import tpu as pltpu
from jax.sharding import PartitionSpec as P

EMB = 256
CODES = 1024
GROUPS = 32
NORM_EPS = 1e-06
SMOOTH_EPS = 1e-05
DECAY = 0.9
MESH = pl.DeviceIdType.MESH

X, Y, Z, CORES = 4, 4, 8, 2
PLANE = X * Y
HALF = CODES // CORES
CHUNK = HALF // PLANE
bf16, f32 = jnp.bfloat16, jnp.float32


def address(x, y, z, core):
    return (((y // 2 * X + x) * Z + z) * CORES + core, y % 2)


def shifts():
    every = [(dx, dy) for dx in range(X) for dy in range(Y) if dx or dy]
    return sorted(every, key=lambda s: -(min(s[0], X - s[0]) + min(s[1], Y - s[1])))


def z_shifts():
    return sorted(range(1, Z), key=lambda d: -min(d, Z - d))


def kernel(
    video_hbm, weight_hbm, gain1_ref, gain2_ref, proj_ref, codes_ref, ema_sum_hbm, ema_count_ref, ones_ref,
    act_hbm, sums_ref, counts_ref, err_ref,
    vid, halo, weight, wide, hid, act2, member, book, ema_sum, lat,
    stat1, stat2, got1, got2, errs, got_err,
    count_own, count_core, count_chip, count_plane, count_z,
    core_out, core_in, half, plane_in, z_buf,
    load_sem, part_send, part_recv, core_sem,
    rs_send, rs_recv, z_send, z_recv, ag_send, ag_recv, fw_send, fw_recv,
    cp_send, cp_recv, cz_send, cz_recv,
):
    clip, strip = lax.axis_index("clip"), lax.axis_index("strip")
    core = clip % CORES
    z = clip // CORES % Z
    x = clip // (CORES * Z) % X
    y = clip // (CORES * Z * X) * 2 + strip
    clips, frames, rows, cols, ch = vid.shape
    per_frame = rows * cols
    per_clip = frames * per_frame
    steps = shifts()
    z_steps = z_shifts()
    partner = (clip, 1 - strip)
    other_core = address(x, y, z, 1 - core)
    plane_peers = [address((x + dx) % X, (y + dy) % Y, z, core) for dx, dy in steps]
    plane_chunks = [(y + dy) % Y * X + (x + dx) % X for dx, dy in steps]
    from_chunks = [(y - dy + Y) % Y * X + (x - dx + X) % X for dx, dy in steps]
    own_chunk = y * X + x
    z_peers = [address(x, y, (z + d) % Z, core) for d in z_steps]

    barrier = pltpu.get_barrier_semaphore()
    everyone = plane_peers + z_peers + [other_core]
    for peer in everyone:
        pl.semaphore_signal(barrier, inc=1, device_id=peer, device_id_type=MESH)

    load_video = [pltpu.make_async_copy(video_hbm.at[c], vid.at[c], load_sem.at[c]) for c in range(clips)]
    for copy in load_video:
        copy.start()
    taps = weight.shape[0]
    skip = weight_hbm.shape[0] - taps
    load_weight = [
        pltpu.make_async_copy(weight_hbm.at[skip + a], weight.at[a], load_sem.at[clips + a]) for a in range(taps)
    ]
    for copy in load_weight:
        copy.start()
    load_sums = pltpu.make_async_copy(ema_sum_hbm, ema_sum, load_sem.at[clips + taps])
    load_sums.start()

    def remote(src, dst, send, recv, peer):
        return pltpu.make_async_remote_copy(
            src_ref=src, dst_ref=dst, send_sem=send, recv_sem=recv, device_id=peer, device_id_type=MESH
        )

    def fold(v):
        return v.reshape(v.shape[0] // 8, 8, v.shape[1]).sum(axis=0)

    block = 128
    for ref in (stat1, stat2, errs):
        ref[...] = jnp.zeros_like(ref)
    for c in range(clips):
        load_video[c].wait()
        first = second = jnp.zeros((8, ch), f32)
        for t in range(frames):
            def add(i, carry, c=c, t=t):
                r = pl.multiple_of(i * (block // cols), block // cols)
                v = vid[c, t, pl.ds(r, block // cols)].reshape(block, ch).astype(f32)
                return carry[0] + fold(v), carry[1] + fold(v * v)
            first, second = lax.fori_loop(0, per_frame // block, add, (first, second), unroll=True)
        stat1[pl.ds(c, 1)] = first.sum(axis=0, keepdims=True)
        stat1[pl.ds(clips + c, 1)] = second.sum(axis=0, keepdims=True)

    pl.semaphore_wait(barrier, len(everyone))
    edge = (rows - 1) * (1 - strip)
    send_halo = remote(video_hbm.at[:, :, pl.ds(edge, 1)], halo, part_send.at[0], part_recv.at[0], partner)
    send_halo.start()
    send_stat1 = remote(stat1, got1, part_send.at[1], part_recv.at[1], partner)
    send_stat1.start()

    span = 128
    tokens = codes_ref.shape[1]

    def mark(i, carry):
        k = pl.multiple_of(i * span, span)
        number = lax.broadcasted_iota(jnp.int32, (span, 256), 0) + k
        total = jnp.zeros((span, 256), f32)
        for j in range(tokens // 256):
            hit = jnp.where(number == codes_ref[:, j * 256:(j + 1) * 256], 1.0, 0.0)
            total += hit
            member[pl.ds(k, span), j * 256:(j + 1) * 256] = hit.astype(bf16)
        lanes = jnp.broadcast_to(total.sum(axis=1, keepdims=True), (span, span))
        count_own[:, pl.ds(k, span)] = lanes.T[:1]
        return carry

    lax.fori_loop(0, CODES // span, mark, 0)
    send_count = remote(count_own, count_core, core_sem.at[0], core_sem.at[1], other_core)
    send_count.start()

    members = per_clip * 2 * (ch // GROUPS)

    def affine(stat, got, gain):
        both = stat[...] + got[...]
        grouped = jnp.dot(both, ones_ref[...], precision=lax.Precision.HIGHEST, preferred_element_type=f32) / members
        centre, square = grouped[:clips], grouped[clips:2 * clips]
        scale = lax.rsqrt(square - centre * centre + NORM_EPS) * gain[...]
        return scale, -centre * scale

    def act(v, scale, shift):
        h = v * (0.5 * scale) + 0.5 * shift
        return h + h * jnp.tanh(h)

    send_stat1.wait()
    scale1, shift1 = affine(stat1, got1, gain1_ref)

    def spread(v, put):
        col = lax.broadcasted_iota(jnp.int32, v.shape, 0) % cols
        put(0, jnp.where(col == 0, 0.0, pltpu.roll(v, 1, 0)).astype(bf16))
        put(1, v.astype(bf16))
        put(2, jnp.where(col == cols - 1, 0.0, pltpu.roll(v, v.shape[0] - 1, 0)).astype(bf16))

    lines = block // cols
    for c in range(clips):
        for t in range(frames):
            def fill(i, carry, c=c, t=t):
                r = i * lines
                v = vid[c, t, pl.ds(r, lines)].reshape(block, ch).astype(f32)
                v = act(v, scale1[c:c + 1], shift1[c:c + 1])

                def put(e, w):
                    wide[c, t, pl.ds(r + 1, lines), :, e * ch:(e + 1) * ch] = w.reshape(lines, cols, ch)

                spread(v, put)
                return carry

            lax.fori_loop(0, rows // lines, fill, 0)

    send_halo.wait()
    near = (rows + 1) * (1 - strip)
    far = (rows + 1) * strip
    for c in range(clips):
        for t in range(frames):
            v = act(halo[c, t].reshape(cols, ch).astype(f32), scale1[c:c + 1], shift1[c:c + 1])

            def put(e, w, c=c, t=t):
                wide[c, t, pl.ds(near, 1), :, e * ch:(e + 1) * ch] = w.reshape(1, cols, ch)

            spread(v, put)
            wide[c, t, pl.ds(far, 1)] = jnp.zeros((1, cols, 3 * ch), bf16)

    send_count.wait()
    count_chip[...] = count_own[...] + count_core[...]
    plane_counts = [
        remote(count_chip, count_plane.at[i], cp_send.at[i], cp_recv.at[i], peer) for i, peer in enumerate(plane_peers)
    ]
    for copy in plane_counts:
        copy.start()

    for copy in load_weight:
        copy.wait()
    last = taps - 1
    for c in range(clips):
        total = None
        for a in range(taps):
            have = frames - (last - a)
            left = jnp.concatenate(
                [wide[c, :have, b:b + rows].reshape(have * per_frame, 3 * ch) for b in range(3)], axis=1
            )
            right = weight[a].reshape(9 * ch, ch)
            part = jnp.dot(left, right, preferred_element_type=f32)
            start = (last - a) * per_frame
            if a == 0:
                hid[c, :start] = vid[c].reshape(per_clip, ch)[:start].astype(f32)
                hid[c, start:] = vid[c].reshape(per_clip, ch)[start:].astype(f32) + part
            else:
                hid[c, start:] = hid[c, start:] + part
        first = second = jnp.zeros((8, ch), f32)

        def add(i, carry, c=c):
            v = hid[c, pl.ds(pl.multiple_of(i * block, block), block)]
            return carry[0] + fold(v), carry[1] + fold(v * v)

        first, second = lax.fori_loop(0, per_clip // block, add, (first, second), unroll=True)
        stat2[pl.ds(c, 1)] = first.sum(axis=0, keepdims=True)
        stat2[pl.ds(clips + c, 1)] = second.sum(axis=0, keepdims=True)

    send_stat2 = remote(stat2, got2, part_send.at[2], part_recv.at[2], partner)
    send_stat2.start()

    total = count_chip[...]
    for i, copy in enumerate(plane_counts):
        copy.wait()
        total = total + count_plane[i]
    count_z[z] = total
    z_counts = [
        remote(count_z.at[z], count_z.at[z], cz_send.at[i], cz_recv.at[i], peer) for i, peer in enumerate(z_peers)
    ]
    for copy in z_counts:
        copy.start()
    load_sums.wait()
    old = ema_count_ref[...]
    n_old = jnp.sum(old)
    smooth = (old + SMOOTH_EPS) / (n_old + CODES * SMOOTH_EPS) * n_old
    for j in range(CODES // span):
        down = jnp.broadcast_to(smooth[:, j * span:(j + 1) * span], (span, span)).T
        entry = ema_sum[j * span:(j + 1) * span] / jnp.concatenate([down] * (EMB // span), axis=1)
        high = entry.astype(bf16)
        book[j * span:(j + 1) * span, :EMB] = high
        book[j * span:(j + 1) * span, EMB:] = (entry - high.astype(f32)).astype(bf16)

    send_stat2.wait()
    scale2, shift2 = affine(stat2, got2, gain2_ref)
    for c in range(clips):
        def second_act(i, carry, c=c):
            r = pl.multiple_of(i * block, block)
            act2[pl.ds(c * per_clip + r, block)] = act(
                hid[c, pl.ds(r, block)], scale2[c:c + 1], shift2[c:c + 1]
            ).astype(bf16)
            return carry

        lax.fori_loop(0, per_clip // block, second_act, 0)

    write_act = pltpu.make_async_copy(act2, act_hbm, load_sem.at[clips + taps + 1])
    write_act.start()

    def sums_of(start):
        mine = jnp.dot(member[pl.ds(start, HALF)], act2[...], preferred_element_type=f32)
        high = mine.astype(bf16)
        low = (mine - high.astype(f32)).astype(bf16)
        return jnp.dot(high, proj_ref[...], preferred_element_type=f32) + jnp.dot(
            low, proj_ref[...], preferred_element_type=f32
        )

    core_out[...] = sums_of(pl.multiple_of((1 - core) * HALF, HALF)).astype(bf16)
    send_core = remote(core_out, core_in, core_sem.at[2], core_sem.at[3], other_core)
    send_core.start()
    lat[:HALF] = sums_of(pl.multiple_of(core * HALF, HALF))
    send_core.wait()
    half_rows = lat[:HALF] + core_in[...].astype(f32)
    lat[:HALF] = half_rows
    half[...] = half_rows.astype(bf16)

    scatter = [
        remote(
            half.at[pl.ds(pl.multiple_of(plane_chunks[i] * CHUNK, CHUNK), CHUNK)],
            plane_in.at[i], rs_send.at[i], rs_recv.at[i], peer,
        )
        for i, peer in enumerate(plane_peers)
    ]
    for copy in scatter:
        copy.start()
    total = lat[pl.ds(pl.multiple_of(own_chunk * CHUNK, CHUNK), CHUNK)]
    for i, copy in enumerate(scatter):
        copy.wait()
        total = total + plane_in[i].astype(f32)

    z_buf[z] = total.astype(bf16)
    along = [remote(z_buf.at[z], z_buf.at[z], z_send.at[i], z_recv.at[i], peer) for i, peer in enumerate(z_peers)]
    for copy in along:
        copy.start()

    for c in range(clips):
        part = jnp.zeros((8, EMB), f32)
        for j in range(per_clip // 256):
            at = c * per_clip + j * 256
            picked = lax.dot_general(
                member[:, at:at + 256], book[...], (((0,), (0,)), ((), ())), preferred_element_type=f32
            )
            value = jnp.dot(act2[at:at + 256], proj_ref[...], preferred_element_type=f32)
            gap = value - (picked[:, :EMB] + picked[:, EMB:])
            part += fold(gap * gap)
        errs[pl.ds(c, 1)] = part.sum(axis=0, keepdims=True)
    send_err = remote(errs, got_err, part_send.at[3], part_recv.at[3], partner)
    send_err.start()

    for copy in along:
        copy.wait()
    total = z_buf[0].astype(f32)
    for i in range(1, Z):
        total = total + z_buf[i].astype(f32)
    base = core * HALF
    own_rows = pl.ds(pl.multiple_of(base + own_chunk * CHUNK, CHUNK), CHUNK)
    sums_ref[own_rows] = total.astype(bf16)
    gather = [
        remote(sums_ref.at[own_rows], sums_ref.at[own_rows], ag_send.at[i], ag_recv.at[i], peer)
        for i, peer in enumerate(plane_peers)
    ]
    for copy in gather:
        copy.start()
    forward = [remote(sums_ref.at[own_rows], sums_ref.at[own_rows], fw_send.at[PLANE - 1], fw_recv.at[PLANE - 1], other_core)]
    forward[0].start()
    for i in reversed(range(PLANE - 1)):
        gather[i].wait_recv()
        here = pl.ds(pl.multiple_of(base + from_chunks[i] * CHUNK, CHUNK), CHUNK)
        copy = remote(sums_ref.at[here], sums_ref.at[here], fw_send.at[i], fw_recv.at[i], other_core)
        copy.start()
        forward.append(copy)

    for copy in z_counts:
        copy.wait()
    total = count_z[0]
    for i in range(1, Z):
        total = total + count_z[i]
    counts_ref[...] = total
    send_err.wait()
    err = (errs[...] + got_err[...]).sum(axis=1, keepdims=True) / (2 * per_clip * EMB)
    err_ref[...] = jnp.broadcast_to(err, err_ref.shape)

    for copy in gather:
        copy.wait_send()
    for copy in forward:
        copy.wait()
    write_act.wait()


def smoothed_book(sums, counts, grand):
    smooth = (counts + SMOOTH_EPS) / (grand + CODES * SMOOTH_EPS) * grand
    return sums / smooth[:, None]


def body(video, gain_first, conv_weight, gain_second, proj_weight, codes, ema_sum, ema_count):
    clips, frames, rows, cols, ch = video.shape
    tokens = clips * frames * rows * cols
    taps = min(frames, conv_weight.shape[0])
    group = ch // GROUPS
    number = jnp.arange(ch) // group
    ones = (number[:, None] == number[None, :]).astype(f32)
    vmem = pl.BlockSpec(memory_space=pltpu.VMEM)
    hbm = pl.BlockSpec(memory_space=pl.ANY)
    near = PLANE - 1
    dma = pltpu.SemaphoreType.DMA
    act2, sums, counts, err = pl.pallas_call(
        kernel,
        out_shape=(
            jax.ShapeDtypeStruct((tokens, ch), bf16),
            jax.ShapeDtypeStruct((CODES, EMB), bf16),
            jax.ShapeDtypeStruct((1, CODES), f32),
            jax.ShapeDtypeStruct((8, 128), f32),
        ),
        in_specs=[hbm, hbm, vmem, vmem, vmem, vmem, hbm, vmem, vmem],
        out_specs=(hbm, vmem, vmem, vmem),
        scratch_shapes=[
            pltpu.VMEM(video.shape, bf16),
            pltpu.VMEM((clips, frames, 1, cols, ch), bf16),
            pltpu.VMEM((taps,) + conv_weight.shape[1:], bf16),
            pltpu.VMEM((clips, frames, rows + 2, cols, 3 * ch), bf16),
            pltpu.VMEM((clips, frames * rows * cols, ch), f32),
            pltpu.VMEM((tokens, ch), bf16),
            pltpu.VMEM((CODES, tokens), bf16),
            pltpu.VMEM((CODES, 2 * EMB), bf16),
            pltpu.VMEM((CODES, EMB), f32),
            pltpu.VMEM((HALF, EMB), f32),
            pltpu.VMEM((8, ch), f32),
            pltpu.VMEM((8, ch), f32),
            pltpu.VMEM((8, ch), f32),
            pltpu.VMEM((8, ch), f32),
            pltpu.VMEM((8, EMB), f32),
            pltpu.VMEM((8, EMB), f32),
            pltpu.VMEM((1, CODES), f32),
            pltpu.VMEM((1, CODES), f32),
            pltpu.VMEM((1, CODES), f32),
            pltpu.VMEM((near, 1, CODES), f32),
            pltpu.VMEM((Z, 1, CODES), f32),
            pltpu.VMEM((HALF, EMB), bf16),
            pltpu.VMEM((HALF, EMB), bf16),
            pltpu.VMEM((HALF, EMB), bf16),
            pltpu.VMEM((near, CHUNK, EMB), bf16),
            pltpu.VMEM((Z, CHUNK, EMB), bf16),
            dma((clips + taps + 2,)),
            dma((4,)), dma((4,)), dma((4,)),
            dma((near,)), dma((near,)), dma((Z - 1,)), dma((Z - 1,)),
            dma((near,)), dma((near,)), dma((PLANE,)), dma((PLANE,)),
            dma((near,)), dma((near,)), dma((Z - 1,)), dma((Z - 1,)),
        ],
        compiler_params=pltpu.CompilerParams(collective_id=0, has_side_effects=True),
    )(
        video, conv_weight, gain_first.reshape(1, -1), gain_second.reshape(1, -1), proj_weight,
        codes.reshape(1, -1), ema_sum, ema_count.reshape(1, -1), ones,
    )
    latent = jnp.dot(act2, proj_weight, preferred_element_type=f32)
    code_count = DECAY * ema_count + (1.0 - DECAY) * counts[0]
    codebook = smoothed_book(
        DECAY * ema_sum + (1.0 - DECAY) * sums.astype(f32), code_count, jnp.sum(code_count)
    )
    return (latent.reshape(video.shape[:4] + (EMB,)), codebook, code_count, err[:clips, 0])


def solution(mesh):
    tiles = P("clip", None, "strip", None, None)
    in_specs = (tiles, P(), P(), P(), P(), P("clip", None, "strip", None), P(), P())
    out_specs = (tiles, P(), P(), P("clip"))
    return jax.shard_map(body, mesh=mesh, in_specs=in_specs, out_specs=out_specs, check_vma=False)
```

time: 392 us -> 57.9 us (0.15)
  waiting for transfers between devices: 166 us -> 0 us
  blocking collectives: 92.3 us -> 0 us
  other arithmetic: 59.1 us -> 3.25 us
  Pallas kernels: 0 us -> 47.1 us
  local copies, waits for them, and re-layouts: 36.3 us -> 2.77 us
  between operations: 15.5 us -> 1.37 us
  matrix products: 12.1 us -> 3.1 us
  starting transfers between devices: 7.6 us -> 0 us
    psum x1 -> x0, waiting for transfers between devices: 160 us -> none  [body(): lax.psum((code_sums, token_counts), ('clip', 'strip'))]
    psum x2 -> x0, blocking collectives: 86.5 us -> none  [the longest x1 82.7 us: body(): lax.psum((code_sums, token_counts), ('clip', 'strip'))]
    pallas_call x0 -> x1, Pallas kernels: none -> 47.1 us  [body(): pl.pallas_call(kernel, out_shape=(jax.ShapeDtypeStruct((tokens, ch), bf16...]
    scatter-add x2 -> x0, other arithmetic: 28.4 us -> none  [the longest x1 15.4 us: body(): jax.ops.segment_sum(jnp.ones(flat_codes.shape, jnp.float32), flat_codes,...]
    reduce_sum x11 -> x1, other arithmetic: 11.4 us -> 0.6 us  [body(): jnp.sum(code_count)]
    conv_general_dilated x1 -> x0, matrix products: 10.3 us -> none  [body(): lax.conv_general_dilated(padded, conv_weight, (1, 1, 1), [(2, 0), (0, 0),...]
    gather x1 -> x0, local copies, waits for them, and re-layouts: 9.78 us -> none  [body(): quantized = jnp.take(old_book, flat_codes, axis=0)]
    all_to_all x1 -> x0, blocking collectives: 5.8 us -> none  [copy_for_each(): lax.all_to_all(jnp.broadcast_to(x[None], (peers, *x.shape)), axis, 0, 0,...]
  transfers between devices with their start and end apart: 4 -> 0, of which waited for: 3 -> 0; matrix products, arithmetic and copies ran while one was open for 6% -> 0% of each run, Pallas kernels for 0% -> 0%
where the time goes in v1:
time: 57.9 us; the launch traced here: 57.6 us
  Pallas kernels  47.1 us (81%)
  other arithmetic  3.25 us (6%)
  matrix products  3.1 us (5%)
  local copies, waits for them, and re-layouts  2.77 us (5%)
  between operations  1.37 us (2%)
    pallas_call x1, Pallas kernels, body(): pl.pallas_call(kernel, out_shape=(jax.ShapeDtypeStruct((tokens, ch), bf16...  47.1 us
    dot_general x1, matrix products, body(): latent = jnp.dot(act2, proj_weight, preferred_element_type=f32)  3.1 us
    reshape x1, local copies, waits for them, and re-layouts, body(): codes.reshape(1, -1)  1.44 us
    slice x1, local copies, waits for them, and re-layouts, body(): err[:clips, 0]  1.3 us
    div x1, other arithmetic, smoothed_book(): return sums / smooth[:, None]  1.18 us

profile of v1, /device:TPU:1, one launch (start us, length us, event | category | flops | bytes accessed | tf_op | source)
XLA Modules:
  0.0 57.6 jit_solution(4645431686119471460)
XLA Ops:
  0.6 1.4 %reshape.54.codes_ref = s32[1,2048]{1,0:T(1,128)} reshape(s32[2,2,16,32]{3,2,1,0:T(8,128)} %param.13) | data formatting | bytes 16384 | tf_op jit(solution)/shard_map/reshape | solution.py:412
  2.1 0.8 %compare_convert_fusion.ones_ref = f32[256,256]{1,0:T(8,128)} fusion(s32[256]{0:T(256)S(1)} %and_select_fusion), kind=kLoop, calls=%fused_computation.1 | loop fusion | flops 131072 | bytes 263168 | tf_op jit(solution)/shard_map/convert_element_type | solution.py:361
  2.9 0.0 copy-start.2
  2.9 47.1 %shard_map.111 = (bf16[2048,256]{1,0:T(8,128)(2,1)}, bf16[1024,256]{1,0:T(8,128)(2,1)}, f32[1,1024]{1,0:T(1,128)}, f32[8,128]{1,0:T(8,128)}) custom-call(bf16[2,2,16,32,256]{4,3,2,1,0:T(8,128)(2,1)} %video_hbm.1, bf16[3,3,3,256,256]{4,3,2,1,0:T(8,128)(2,1)} %weight_hbm.1, f32[1,256]{1,0:T(1,128)} %bitcast.12, f32[1,256]{1,0:T(1,128)} %bitcast.13, ...), custom_call_target="tpu_custom_call" | custom-call | tf_op jit(solution)/shard_map/pallas_call | solution.py:366
  50.0 0.0 copy-start.5
  50.0 0.0 copy-start.3
  50.0 0.0 copy-start
  50.1 0.0 copy-start.1
  50.1 0.0 copy-done.2
  50.1 3.1 %fusion.1 = f32[2048,256]{1,0:T(8,128)} fusion(bf16[2048,256]{1,0:T(8,128)(2,1)} %get-tuple-element.8, bf16[256,256]{1,0:T(8,128)(2,1)S(1)} %copy-done.2), kind=kOutput, calls=%fused_computation.11 | convolution fusion | flops 268435456 | bytes 3276800 | tf_op jit(solution)/shard_map/dot_general | solution.py:414
  53.2 0.0 copy-done.5
  53.2 0.0 copy-done.3
  53.2 0.6 %fusion = (f32[]{:T(128)}, f32[1024]{0:T(1024)S(1)}) fusion(f32[1024]{0:T(1024)S(1)} %bitcast.11, f32[1024]{0:T(1024)S(1)} %copy-done.3), kind=kLoop, calls=%fused_computation.10 | loop fusion | flops 3071 | bytes 12292 | tf_op jit(solution)/shard_map/reduce_sum | solution.py:417
  53.8 0.0 copy-start.4
  54.5 0.7 %divide_multiply_fusion = f32[1024]{0:T(1024)S(1)} fusion(f32[1024]{0:T(1024)S(1)} %get-tuple-element.13, f32[]{:T(128)} %get-tuple-element.12, f32[]{:T(128)S(6)} %add.28), kind=kLoop, calls=%fused_computation.2 | loop fusion | flops 3072 | bytes 8200 | tf_op jit(solution)/shard_map/mul | solution.py:351
  55.1 0.0 copy-done
  55.1 0.0 copy-done.1
  55.1 1.2 %add_divide_fusion = f32[1024,256]{1,0:T(8,128)} fusion(bf16[1024,256]{1,0:T(8,128)(2,1)S(1)} %copy-done.1, f32[1024,256]{1,0:T(8,128)S(1)} %copy-done, f32[1024]{0:T(1024)S(1)} %divide_multiply_fusion), kind=kLoop, calls=%fused_computation | loop fusion | flops 1310720 | bytes 2625536 | tf_op jit(solution)/shard_map/div | solution.py:352
  56.3 1.3 %slice_reduce_fusion = f32[2]{0:T(128)} fusion(f32[8,128]{1,0:T(8,128)} %get-tuple-element.11), kind=kLoop, calls=%fused_computation.9 | loop fusion | bytes 16 | tf_op jit(solution)/shard_map/slice | solution.py:419
  57.6 0.0 copy-done.4
  (2 shorter events, 0.0 us)
Async XLA Ops:
  2.9 47.2 %copy-start.2 = (bf16[256,256]{1,0:T(8,128)(2,1)S(1)}, bf16[256,256]{1,0:T(8,128)(2,1)}, u32[]{:S(2)}) copy-start(bf16[256,256]{1,0:T(8,128)(2,1)} %proj_ref.1) | copy-start | bytes 393220
  50.0 3.2 %copy-start.5 = (f32[1,1024]{1,0:T(1,128)S(1)}, f32[1,1024]{1,0:T(1,128)}, u32[]{:S(2)}) copy-start(f32[1,1024]{1,0:T(1,128)} %get-tuple-element.10) | copy-start | bytes 12292
  50.0 3.2 %copy-start.3 = (f32[1024]{0:T(1024)S(1)}, f32[1024]{0:T(1024)}, u32[]{:S(2)}) copy-start(f32[1024]{0:T(1024)} %param.15) | copy-start | bytes 12292
  50.0 5.1 %copy-start = (f32[1024,256]{1,0:T(8,128)S(1)}, f32[1024,256]{1,0:T(8,128)}, u32[]{:S(2)}) copy-start(f32[1024,256]{1,0:T(8,128)} %ema_sum_hbm.1) | copy-start | bytes 3145732
  50.1 5.1 %copy-start.1 = (bf16[1024,256]{1,0:T(8,128)(2,1)S(1)}, bf16[1024,256]{1,0:T(8,128)(2,1)}, u32[]{:S(2)}) copy-start(bf16[1024,256]{1,0:T(8,128)(2,1)} %get-tuple-element.9) | copy-start | bytes 1572868
  53.8 3.8 %copy-start.4 = (f32[1024]{0:T(1024)}, f32[1024]{0:T(1024)S(1)}, u32[]{:S(2)}) copy-start(f32[1024]{0:T(1024)S(1)} %get-tuple-element.13) | copy-start | bytes 12292

commit v2 on v1

v2 whole, which is shorter than its diff:
```python
import jax
import jax.numpy as jnp
from jax import lax
from jax.experimental import pallas as pl
from jax.experimental.pallas import tpu as pltpu
from jax.sharding import PartitionSpec as P

EMB = 256
CODES = 1024
GROUPS = 32
NORM_EPS = 1e-06
SMOOTH_EPS = 1e-05
DECAY = 0.9
MESH = pl.DeviceIdType.MESH

X, Y, Z, CORES = 4, 4, 8, 2
PLANE = X * Y
HALF = CODES // CORES
WAVES = 2
WAVE = HALF // WAVES
CHUNK = WAVE // PLANE
NEAR = PLANE - 1
SPAN = 128
bf16, f32 = jnp.bfloat16, jnp.float32


def address(x, y, z, core):
    return (((y // 2 * X + x) * Z + z) * CORES + core, y % 2)


def shifts():
    every = [(dx, dy) for dx in range(X) for dy in range(Y) if dx or dy]
    return sorted(every, key=lambda s: -(min(s[0], X - s[0]) + min(s[1], Y - s[1])))


def z_shifts():
    return sorted(range(1, Z), key=lambda d: -min(d, Z - d))


def ds(start, size):
    return pl.ds(pl.multiple_of(start, size), size)


def fold(v):
    return v.reshape(v.shape[0] // 8, 8, v.shape[1]).sum(axis=0)


def down(row):
    return jnp.broadcast_to(row, (SPAN, SPAN)).T


def smoothed(counts):
    grand = jnp.sum(counts)
    return (counts + SMOOTH_EPS) / (grand + CODES * SMOOTH_EPS) * grand


def kernel(
    video_hbm, weight_hbm, gain1_hbm, gain2_hbm, proj_hbm, codes_hbm, ema_sum_hbm, ema_count_hbm,
    act_hbm, sums_ref, counts_ref, err_ref,
    vid, halo, weight, wide, hid, act2, member, book, ema_sum, raw, codes_in, codes_at,
    gain1_ref, gain2_ref, proj_ref, ema_count_ref,
    stat1, stat2, got1, got2, errs, got_err,
    count_own, count_core, count_chip, count_plane, count_z,
    core_out, core_in, half, plane_in, z_buf,
    load_sem, part_send, part_recv, cc_sem, core_send, core_recv,
    rs_send, rs_recv, z_send, z_recv, ag_send, ag_recv, fw_send, fw_recv,
    cp_sem, cz_sem,
):
    clips, frames, rows, cols, ch = vid.shape
    per_frame = rows * cols
    per_clip = frames * per_frame
    taps = weight.shape[0]
    skip = weight_hbm.shape[0] - taps

    def load(src, dst, i):
        copy = pltpu.make_async_copy(src, dst, load_sem.at[i])
        copy.start()
        return copy

    load_video = [load(video_hbm.at[c], vid.at[c], c) for c in range(clips)]
    load_codes = load(codes_hbm, codes_in, clips)
    load_small = [
        load(src, dst, clips + 1 + i)
        for i, (src, dst) in enumerate(
            [(gain1_hbm, gain1_ref), (gain2_hbm, gain2_ref), (ema_count_hbm, ema_count_ref), (proj_hbm, proj_ref)]
        )
    ]
    load_weight = [load(weight_hbm.at[skip + a], weight.at[a], clips + 5 + a) for a in range(taps)]

    clip, strip = lax.axis_index("clip"), lax.axis_index("strip")
    core = clip % CORES
    z = clip // CORES % Z
    x = clip // (CORES * Z) % X
    y = clip // (CORES * Z * X) * 2 + strip
    steps = shifts()
    z_steps = z_shifts()
    partner = (clip, 1 - strip)
    other_core = address(x, y, z, 1 - core)
    plane_peers = [address((x + dx) % X, (y + dy) % Y, z, core) for dx, dy in steps]
    plane_chunks = [(y + dy) % Y * X + (x + dx) % X for dx, dy in steps]
    own_chunk = y * X + x
    z_peers = [address(x, y, (z + d) % Z, core) for d in z_steps]

    barrier = pltpu.get_barrier_semaphore()
    everyone = plane_peers + z_peers + [other_core]
    for peer in everyone:
        pl.semaphore_signal(barrier, inc=1, device_id=peer, device_id_type=MESH)

    def remote(src, dst, send, recv, peer):
        return pltpu.make_async_remote_copy(
            src_ref=src, dst_ref=dst, send_sem=send, recv_sem=recv, device_id=peer, device_id_type=MESH
        )

    def push(src, dst, send, recv, peer):
        copy = remote(src, dst, send, recv, peer)
        copy.start()
        return copy

    block = 128
    lines = block // cols
    for ref in (stat1, stat2, errs):
        ref[...] = jnp.zeros_like(ref)
    for c in range(clips):
        load_video[c].wait()
        first = second = jnp.zeros((8, ch), f32)
        for t in range(frames):
            def add(i, carry, c=c, t=t):
                r = pl.multiple_of(i * lines, lines)
                v = vid[c, t, pl.ds(r, lines)].reshape(block, ch).astype(f32)
                return carry[0] + fold(v), carry[1] + fold(v * v)
            first, second = lax.fori_loop(0, per_frame // block, add, (first, second), unroll=True)
        stat1[pl.ds(c, 1)] = first.sum(axis=0, keepdims=True)
        stat1[pl.ds(clips + c, 1)] = second.sum(axis=0, keepdims=True)

    pl.semaphore_wait(barrier, len(everyone))
    send_stat1 = push(stat1, got1, part_send.at[0], part_recv.at[0], partner)
    edge = (rows - 1) * (1 - strip)
    send_halo = push(video_hbm.at[:, :, pl.ds(edge, 1)], halo, part_send.at[1], part_recv.at[1], partner)

    load_codes.wait()
    quads = rows // lines
    for c in range(clips):
        for t in range(frames):
            codes_at[pl.ds((c * frames + t) * quads, quads)] = jnp.concatenate(
                [codes_in[c, t, pl.ds(p, quads, stride=lines)] for p in range(lines)], axis=1
            )
    blocks = clips * frames * quads

    def mark(i, carry):
        k = pl.multiple_of(i * SPAN, SPAN)
        number = lax.broadcasted_iota(jnp.int32, (SPAN, block), 0) + k
        total = jnp.zeros((SPAN, block), f32)
        for j in range(blocks):
            hit = jnp.where(number == codes_at[j:j + 1], 1.0, 0.0)
            total += hit
            member[pl.ds(k, SPAN), j * block:(j + 1) * block] = hit.astype(bf16)
        lanes = jnp.broadcast_to(total.sum(axis=1, keepdims=True), (SPAN, SPAN))
        count_own[:, pl.ds(k, SPAN)] = lanes.T[:1]
        return carry

    lax.fori_loop(0, CODES // SPAN, mark, 0)
    send_count = push(count_own, count_core, cc_sem.at[0], cc_sem.at[1], other_core)

    members = per_clip * 2 * (ch // GROUPS)
    group = ch // GROUPS
    same = (
        lax.broadcasted_iota(jnp.int32, (ch, ch), 0) // group == lax.broadcasted_iota(jnp.int32, (ch, ch), 1) // group
    )
    ones = jnp.where(same, 1.0, 0.0).astype(f32)

    def affine(both, count, gain):
        grouped = jnp.dot(both, ones, precision=lax.Precision.HIGHEST, preferred_element_type=f32) / members
        centre, square = grouped[:count], grouped[count:2 * count]
        scale = lax.rsqrt(square - centre * centre + NORM_EPS) * gain[...]
        return scale, -centre * scale

    def act(v, scale, shift):
        h = v * (0.5 * scale) + 0.5 * shift
        return h + h * jnp.tanh(h)

    for copy in load_small:
        copy.wait()
    send_stat1.wait()
    scale1, shift1 = affine(stat1[...] + got1[...], clips, gain1_ref)

    def spread(v, put):
        col = lax.broadcasted_iota(jnp.int32, v.shape, 0) % cols
        put(0, jnp.where(col == 0, 0.0, pltpu.roll(v, 1, 0)).astype(bf16))
        put(1, v.astype(bf16))
        put(2, jnp.where(col == cols - 1, 0.0, pltpu.roll(v, v.shape[0] - 1, 0)).astype(bf16))

    for c in range(clips):
        for t in range(frames):
            def fill(i, carry, c=c, t=t):
                r = i * lines
                v = vid[c, t, pl.ds(r, lines)].reshape(block, ch).astype(f32)
                v = act(v, scale1[c:c + 1], shift1[c:c + 1])

                def put(e, w):
                    wide[c, t, pl.ds(r + 1, lines), :, e * ch:(e + 1) * ch] = w.reshape(lines, cols, ch)

                spread(v, put)
                return carry

            lax.fori_loop(0, rows // lines, fill, 0)

    send_halo.wait()
    near = (rows + 1) * (1 - strip)
    far = (rows + 1) * strip
    for c in range(clips):
        for t in range(frames):
            v = act(halo[c, t].reshape(cols, ch).astype(f32), scale1[c:c + 1], shift1[c:c + 1])

            def put(e, w, c=c, t=t):
                wide[c, t, pl.ds(near, 1), :, e * ch:(e + 1) * ch] = w.reshape(1, cols, ch)

            spread(v, put)
            wide[c, t, pl.ds(far, 1)] = jnp.zeros((1, cols, 3 * ch), bf16)

    send_count.wait()
    count_chip[...] = count_own[...] + count_core[...]
    plane_counts = [
        push(count_chip, count_plane.at[i], cp_sem.at[0], cp_sem.at[1], peer) for i, peer in enumerate(plane_peers)
    ]

    for copy in load_weight:
        copy.wait()
    load_sums = load(ema_sum_hbm, ema_sum, clips + 5 + taps)
    last = taps - 1
    send_stat2 = []
    for c in range(clips):
        for a in range(taps):
            have = frames - (last - a)
            left = jnp.concatenate(
                [wide[c, :have, b:b + rows].reshape(have * per_frame, 3 * ch) for b in range(3)], axis=1
            )
            right = weight[a].reshape(9 * ch, ch)
            part = jnp.dot(left, right, preferred_element_type=f32)
            start = (last - a) * per_frame
            if a == 0:
                hid[c, :start] = vid[c].reshape(per_clip, ch)[:start].astype(f32)
                hid[c, start:] = vid[c].reshape(per_clip, ch)[start:].astype(f32) + part
            else:
                hid[c, start:] = hid[c, start:] + part

        def add(i, carry, c=c):
            v = hid[c, ds(i * block, block)]
            return carry[0] + fold(v), carry[1] + fold(v * v)

        zero = jnp.zeros((8, ch), f32)
        first, second = lax.fori_loop(0, per_clip // block, add, (zero, zero), unroll=True)
        stat2[c, 0:1] = first.sum(axis=0, keepdims=True)
        stat2[c, 1:2] = second.sum(axis=0, keepdims=True)
        send_stat2.append(push(stat2.at[c], got2.at[c], part_send.at[2 + c], part_recv.at[2 + c], partner))

    every_count = remote(count_plane, count_plane, cp_sem.at[0], cp_sem.at[1], partner)
    every_count.wait()
    total = count_chip[...]
    for i in range(NEAR):
        total = total + count_plane[i]
    count_z[z] = total
    for peer in z_peers:
        push(count_z.at[z], count_z.at[z], cz_sem.at[0], cz_sem.at[1], peer)

    far_half, own_half = ds((1 - core) * HALF, HALF), ds(core * HALF, HALF)
    for c in range(clips):
        send_stat2[c].wait()
        scale2, shift2 = affine(stat2[c] + got2[c], 1, gain2_ref)

        def second_act(i, carry, c=c):
            r = pl.multiple_of(i * block, block)
            act2[pl.ds(c * per_clip + r, block)] = act(hid[c, pl.ds(r, block)], scale2, shift2).astype(bf16)
            return carry

        lax.fori_loop(0, per_clip // block, second_act, 0)
        if c < clips - 1:
            mine = act2[c * per_clip:(c + 1) * per_clip]
            for i, place in enumerate((far_half, own_half)):
                part = jnp.dot(
                    member[place, c * per_clip:(c + 1) * per_clip], mine, preferred_element_type=f32
                )
                raw[i] = part if c == 0 else raw[i] + part

    write_act = load(act2, act_hbm, clips + 6 + taps)

    def sums_of(i, w):
        start = ((1 - core) if i == 0 else core) * HALF + w * WAVE
        c = clips - 1
        mine = raw[i, w * WAVE:(w + 1) * WAVE] + jnp.dot(
            member[ds(start, WAVE), c * per_clip:(c + 1) * per_clip],
            act2[c * per_clip:(c + 1) * per_clip], preferred_element_type=f32,
        )
        high = mine.astype(bf16)
        low = (mine - high.astype(f32)).astype(bf16)
        return jnp.dot(high, proj_ref[...], preferred_element_type=f32) + jnp.dot(
            low, proj_ref[...], preferred_element_type=f32
        )

    send_core = []
    for w in range(WAVES):
        core_out[w] = sums_of(0, w).astype(bf16)
        send_core.append(push(core_out.at[w], core_in.at[w], core_send.at[w], core_recv.at[w], other_core))
    for w in range(WAVES):
        own = sums_of(1, w)
        send_core[w].wait()
        own = own + core_in[w].astype(f32)
        raw[1, w * WAVE:(w + 1) * WAVE] = own
        half[w] = own.astype(bf16)
        for i, peer in enumerate(plane_peers):
            push(half.at[w, ds(plane_chunks[i] * CHUNK, CHUNK)], plane_in.at[w, i], rs_send.at[w], rs_recv.at[w], peer)

    for w in range(WAVES):
        remote(plane_in.at[w], plane_in.at[w], rs_send.at[w], rs_recv.at[w], partner).wait()
        total = raw[1, ds(w * WAVE + own_chunk * CHUNK, CHUNK)]
        for i in range(NEAR):
            total = total + plane_in[w, i].astype(f32)
        z_buf[w, z] = total.astype(bf16)
        for peer in z_peers:
            push(z_buf.at[w, z], z_buf.at[w, z], z_send.at[w], z_recv.at[w], peer)

    load_sums.wait()
    smooth = smoothed(ema_count_ref[...])
    for j in range(CODES // SPAN):
        scale = jnp.concatenate([down(smooth[:, j * SPAN:(j + 1) * SPAN])] * (EMB // SPAN), axis=1)
        entry = ema_sum[j * SPAN:(j + 1) * SPAN] / scale
        high = entry.astype(bf16)
        book[j * SPAN:(j + 1) * SPAN, :EMB] = high
        book[j * SPAN:(j + 1) * SPAN, EMB:] = (entry - high.astype(f32)).astype(bf16)

    def distances(c):
        part = jnp.zeros((8, EMB), f32)
        for j in range(per_clip // 256):
            at = c * per_clip + j * 256
            picked = lax.dot_general(
                member[:, at:at + 256], book[...], (((0,), (0,)), ((), ())), preferred_element_type=f32
            )
            value = jnp.dot(act2[at:at + 256], proj_ref[...], preferred_element_type=f32)
            gap = value - (picked[:, :EMB] + picked[:, EMB:])
            part += fold(gap * gap)
        errs[pl.ds(c, 1)] = part.sum(axis=0, keepdims=True)

    for c in range(clips):
        distances(c)
    send_err = push(errs, got_err, part_send.at[2 + clips], part_recv.at[2 + clips], partner)

    base = core * HALF
    for w in range(WAVES):
        arrived = z_buf.at[w, pl.ds(0, Z - 1)]
        remote(arrived, arrived, z_send.at[w], z_recv.at[w], partner).wait()
        total = z_buf[w, 0].astype(f32)
        for i in range(1, Z):
            total = total + z_buf[w, i].astype(f32)
        own_rows = ds(base + w * WAVE + own_chunk * CHUNK, CHUNK)
        sums_ref[own_rows] = total.astype(bf16)
        for peer in plane_peers:
            push(sums_ref.at[own_rows], sums_ref.at[own_rows], ag_send.at[w], ag_recv.at[w], peer)

    arrived = count_z.at[pl.ds(0, Z - 1)]
    remote(arrived, arrived, cz_sem.at[0], cz_sem.at[1], partner).wait()
    total = count_z[0]
    for i in range(1, Z):
        total = total + count_z[i]
    counts_ref[...] = total
    send_err.wait()
    err = (errs[...] + got_err[...]).sum(axis=1, keepdims=True) / (2 * per_clip * EMB)
    err_ref[...] = jnp.broadcast_to(err, err_ref.shape)

    forward = []
    for w in range(WAVES):
        remote(plane_in.at[w], plane_in.at[w], ag_send.at[w], ag_recv.at[w], partner).wait()
        here = ds(base + w * WAVE, WAVE)
        forward.append(push(sums_ref.at[here], sums_ref.at[here], fw_send.at[w], fw_recv.at[w], other_core))
    for copy in forward:
        copy.wait()
    write_act.wait()


def finish(
    act_hbm, sums_hbm, counts_hbm, ema_sum_hbm, ema_count_hbm, proj_hbm, err_hbm,
    latent_hbm, book_hbm, count_ref, err_out,
    act2, sums, counts, ema_sum, ema_count, proj, err, latent, book, in_sem, out_sem,
):
    tokens = act2.shape[0]
    parts = 4
    step = tokens // parts
    turn = CODES // parts

    def load(src, dst, i):
        copy = pltpu.make_async_copy(src, dst, in_sem.at[i])
        copy.start()
        return copy

    small = [
        load(src, dst, i)
        for i, (src, dst) in enumerate(
            [(proj_hbm, proj), (counts_hbm, counts), (ema_count_hbm, ema_count), (err_hbm, err)]
        )
    ]
    acts = [load(act_hbm.at[pl.ds(i * step, step)], act2.at[pl.ds(i * step, step)], 4 + i) for i in range(parts)]
    terms = [load(sums_hbm, sums, 4 + parts), load(ema_sum_hbm, ema_sum, 5 + parts)]
    for copy in small:
        copy.wait()
    out = []

    def put(src, dst):
        copy = pltpu.make_async_copy(src, dst, out_sem.at[len(out)])
        copy.start()
        out.append(copy)

    for i in range(parts):
        acts[i].wait()
        at = pl.ds(i * step, step)
        latent[at] = jnp.dot(act2[at], proj[...], preferred_element_type=f32)
        put(latent.at[at], latent_hbm.at[at])
    code_count = DECAY * ema_count[...] + (1.0 - DECAY) * counts[...]
    count_ref[...] = code_count
    smooth = smoothed(code_count)
    for i in range(err_out.shape[0]):
        err_out[i] = err[i, 0]
    for copy in terms:
        copy.wait()
    for i in range(parts):
        for j in range(i * turn // SPAN, (i + 1) * turn // SPAN):
            at = pl.ds(j * SPAN, SPAN)
            scale = jnp.concatenate([down(smooth[:, j * SPAN:(j + 1) * SPAN])] * (EMB // SPAN), axis=1)
            book[at] = (DECAY * ema_sum[at] + (1.0 - DECAY) * sums[at].astype(f32)) / scale
        at = pl.ds(i * turn, turn)
        put(book.at[at], book_hbm.at[at])
    for copy in out:
        copy.wait()


def body(video, gain_first, conv_weight, gain_second, proj_weight, codes, ema_sum, ema_count):
    clips, frames, rows, cols, ch = video.shape
    tokens = clips * frames * rows * cols
    taps = min(frames, conv_weight.shape[0])
    vmem = pl.BlockSpec(memory_space=pltpu.VMEM)
    near = pl.BlockSpec(memory_space=pl.ANY)
    hbm = pl.BlockSpec(memory_space=pltpu.HBM)
    dma = pltpu.SemaphoreType.DMA
    V = pltpu.VMEM
    count_row = ema_count.reshape(1, -1)
    keep = lambda a: pltpu.with_memory_space_constraint(a, pltpu.HBM)
    video, conv_weight, proj_weight, codes, ema_sum, count_row = map(keep, (video, conv_weight, proj_weight, codes, ema_sum, count_row))
    gain_first, gain_second = keep(gain_first.reshape(1,-1)), keep(gain_second.reshape(1,-1))
    act2, sums, counts, err = pl.pallas_call(
        kernel,
        out_shape=(
            jax.ShapeDtypeStruct((tokens, ch), bf16),
            jax.ShapeDtypeStruct((CODES, EMB), bf16),
            jax.ShapeDtypeStruct((1, CODES), f32),
            jax.ShapeDtypeStruct((8, 128), f32),
        ),
        in_specs=[hbm] * 8,
        out_specs=(near, vmem, vmem, vmem),
        scratch_shapes=[
            V(video.shape, bf16),
            V((clips, frames, 1, cols, ch), bf16),
            V((taps,) + conv_weight.shape[1:], bf16),
            V((clips, frames, rows + 2, cols, 3 * ch), bf16),
            V((clips, frames * rows * cols, ch), f32),
            V((tokens, ch), bf16),
            V((CODES, tokens), bf16),
            V((CODES, 2 * EMB), bf16),
            V((CODES, EMB), f32),
            V((2, HALF, EMB), f32),
            V(codes.shape, jnp.int32),
            V((tokens // 128, 128), jnp.int32),
            V((1, ch), f32), V((1, ch), f32), V(proj_weight.shape, bf16), V((1, CODES), f32),
            V((8, ch), f32), V((clips, 8, ch), f32), V((8, ch), f32), V((clips, 8, ch), f32),
            V((8, EMB), f32), V((8, EMB), f32),
            V((1, CODES), f32), V((1, CODES), f32), V((1, CODES), f32),
            V((NEAR, 1, CODES), f32), V((Z, 1, CODES), f32),
            V((WAVES, WAVE, EMB), bf16), V((WAVES, WAVE, EMB), bf16), V((WAVES, WAVE, EMB), bf16),
            V((WAVES, NEAR, CHUNK, EMB), bf16), V((WAVES, Z, CHUNK, EMB), bf16),
            dma((clips + taps + 7,)),
            dma((clips + 3,)), dma((clips + 3,)), dma((2,)),
        ] + [dma((WAVES,))] * 10 + [dma((2,))] * 2,
        compiler_params=pltpu.CompilerParams(
            collective_id=0, has_side_effects=True, vmem_limit_bytes=32 << 20
        ),
    )(
        video, conv_weight, gain_first.reshape(1, -1), gain_second.reshape(1, -1), proj_weight,
        codes, ema_sum, count_row,
    )
    latent, codebook, code_count, clip_error = pl.pallas_call(
        finish,
        out_shape=(
            jax.ShapeDtypeStruct((tokens, EMB), f32),
            jax.ShapeDtypeStruct((CODES, EMB), f32),
            jax.ShapeDtypeStruct((1, CODES), f32),
            jax.ShapeDtypeStruct((clips,), f32),
        ),
        in_specs=[near, near, near, hbm, hbm, hbm, near],
        out_specs=(hbm, hbm, vmem, pl.BlockSpec(memory_space=pltpu.SMEM)),
        scratch_shapes=[
            V((tokens, ch), bf16), V((CODES, EMB), bf16), V((1, CODES), f32), V((CODES, EMB), f32),
            V((1, CODES), f32), V(proj_weight.shape, bf16), V((8, 128), f32),
            V((tokens, EMB), f32), V((CODES, EMB), f32), dma((10,)), dma((8,)),
        ],
        compiler_params=pltpu.CompilerParams(vmem_limit_bytes=16 << 20),
    )(act2, sums, counts, ema_sum, count_row, proj_weight, err)
    return (latent.reshape(video.shape[:4] + (EMB,)), codebook, code_count.reshape(-1), clip_error)


def solution(mesh):
    tiles = P("clip", None, "strip", None, None)
    in_specs = (tiles, P(), P(), P(), P(), P("clip", None, "strip", None), P(), P())
    out_specs = (tiles, P(), P(), P("clip"))
    return jax.shard_map(body, mesh=mesh, in_specs=in_specs, out_specs=out_specs, check_vma=False)
```

time: 57.9 us -> 50 us (0.86)
  other arithmetic: 3.25 us -> 0 us
  matrix products: 3.1 us -> 0 us
  local copies, waits for them, and re-layouts: 2.77 us -> 0 us
  Pallas kernels: 47.1 us -> 49.3 us
  between operations: 1.37 us -> 0.64 us
    pallas_call x0 -> x1, Pallas kernels: none -> 3.95 us  [body(): pl.pallas_call(finish, out_shape=(jax.ShapeDtypeStruct((tokens, EMB), f32...]
    dot_general x1 -> x0, matrix products: 3.1 us -> none  [body(): latent = jnp.dot(act2, proj_weight, preferred_element_type=f32)]
    pallas_call x1, Pallas kernels: 47.1 us -> 45.3 us  [body(): pl.pallas_call(kernel, out_shape=(jax.ShapeDtypeStruct((tokens, ch), bf16...]
    reshape x1 -> x0, local copies, waits for them, and re-layouts: 1.44 us -> none  [body(): codes.reshape(1, -1)]
    slice x1 -> x0, local copies, waits for them, and re-layouts: 1.3 us -> none  [body(): err[:clips, 0]]
    div x1 -> x0, other arithmetic: 1.18 us -> none  [smoothed_book(): return sums / smooth[:, None]]
    convert_element_type x1 -> x0, other arithmetic: 0.81 us -> none  [body(): ones = (number[:, None] == number[None, :]).astype(f32)]
    mul x2 -> x0, other arithmetic: 0.66 us -> none  [the longest x1 0.65 us: smoothed_book(): smooth = (counts + SMOOTH_EPS) / (grand + CODES * SMOOTH_EPS) * grand]
where the time goes in v2:
time: 50 us; the launch traced here: 49.9 us
  Pallas kernels  49.3 us (99%)
  between operations  0.64 us (1%)
    pallas_call x1, Pallas kernels, body(): pl.pallas_call(kernel, out_shape=(jax.ShapeDtypeStruct((tokens, ch), bf16...  45.3 us
    pallas_call x1, Pallas kernels, body(): pl.pallas_call(finish, out_shape=(jax.ShapeDtypeStruct((tokens, EMB), f32...  3.95 us

profile of v2, /device:TPU:1, one launch (start us, length us, event | category | flops | bytes accessed | tf_op | source)
XLA Modules:
  0.0 49.9 jit_solution(11626642978217408836)
XLA Ops:
  0.6 45.3 %shard_map.111 = (bf16[2048,256]{1,0:T(8,128)(2,1)S(1)}, bf16[1024,256]{1,0:T(8,128)(2,1)S(1)}, f32[1,1024]{1,0:T(1,128)S(1)}, f32[8,128]{1,0:T(8,128)S(1)}) custom-call(bf16[2,2,16,32,256]{4,3,2,1,0:T(8,128)(2,1)} %video_hbm.1, bf16[3,3,3,256,256]{4,3,2,1,0:T(8,128)(2,1)} %weight_hbm.1, f32[1,256]{1,0:T(1,128)} %bitcast.7, f32[1,256]{1,0:T(1,128)} %bitcast.8, ...), custom_call_target="tpu_custom_call" | custom-call | tf_op jit(solution)/shard_map/pallas_call | solution.py:446
  46.0 4.0 %shard_map.112 = (f32[2048,256]{1,0:T(8,128)}, f32[1024,256]{1,0:T(8,128)}, f32[1,1024]{1,0:T(1,128)}, f32[2]{0:T(128)}) custom-call(bf16[2048,256]{1,0:T(8,128)(2,1)S(1)} %get-tuple-element.12.act_hbm, bf16[1024,256]{1,0:T(8,128)(2,1)S(1)} %get-tuple-element.13.sums_hbm, f32[1,1024]{1,0:T(1,128)S(1)} %get-tuple-element.14.counts_hbm, ...), custom_call_target="tpu_custom_call" | custom-call | tf_op jit(solution)/shard_map/pallas_call | solution.py:486

commit v3 on v2

--- a/solution.py
+++ b/solution.py
@@ -21,6 +21,7 @@
 CHUNK = WAVE // PLANE
 NEAR = PLANE - 1
 SPAN = 128
+PIECES = 2
 bf16, f32 = jnp.bfloat16, jnp.float32
 
 
@@ -56,8 +57,8 @@
 
 def kernel(
     video_hbm, weight_hbm, gain1_hbm, gain2_hbm, proj_hbm, codes_hbm, ema_sum_hbm, ema_count_hbm,
-    act_hbm, sums_ref, counts_ref, err_ref,
-    vid, halo, weight, wide, hid, act2, member, book, ema_sum, raw, codes_in, codes_at,
+    latent, ema_sum, sums_ref, counts_ref, err_ref,
+    vid, halo, weight, wide, hid, act2, member, book, raw, codes_in, codes_at,
     gain1_ref, gain2_ref, proj_ref, ema_count_ref,
     stat1, stat2, got1, got2, errs, got_err,
     count_own, count_core, count_chip, count_plane, count_z,
@@ -144,22 +145,24 @@
             codes_at[pl.ds((c * frames + t) * quads, quads)] = jnp.concatenate(
                 [codes_in[c, t, pl.ds(p, quads, stride=lines)] for p in range(lines)], axis=1
             )
-    blocks = clips * frames * quads
-
-    def mark(i, carry):
-        k = pl.multiple_of(i * SPAN, SPAN)
-        number = lax.broadcasted_iota(jnp.int32, (SPAN, block), 0) + k
-        total = jnp.zeros((SPAN, block), f32)
-        for j in range(blocks):
-            hit = jnp.where(number == codes_at[j:j + 1], 1.0, 0.0)
-            total += hit
-            member[pl.ds(k, SPAN), j * block:(j + 1) * block] = hit.astype(bf16)
-        lanes = jnp.broadcast_to(total.sum(axis=1, keepdims=True), (SPAN, SPAN))
-        count_own[:, pl.ds(k, SPAN)] = lanes.T[:1]
-        return carry
-
-    lax.fori_loop(0, CODES // SPAN, mark, 0)
-    send_count = push(count_own, count_core, cc_sem.at[0], cc_sem.at[1], other_core)
+    def mark(c):
+        first, end = c * frames * quads, (c + 1) * frames * quads
+
+        def some(i, carry):
+            k = pl.multiple_of(i * SPAN, SPAN)
+            number = lax.broadcasted_iota(jnp.int32, (SPAN, block), 0) + k
+            total = jnp.zeros((SPAN, block), f32)
+            for j in range(first, end):
+                hit = jnp.where(number == codes_at[j:j + 1], 1.0, 0.0)
+                total += hit
+                member[pl.ds(k, SPAN), j * block:(j + 1) * block] = hit.astype(bf16)
+            found = jnp.broadcast_to(total.sum(axis=1, keepdims=True), (SPAN, SPAN)).T[:1]
+            count_own[:, pl.ds(k, SPAN)] = found if c == 0 else count_own[:, pl.ds(k, SPAN)] + found
+            return carry
+
+        lax.fori_loop(0, CODES // SPAN, some, 0)
+
+    mark(0)
 
     members = per_clip * 2 * (ch // GROUPS)
     group = ch // GROUPS
@@ -217,31 +220,30 @@
             spread(v, put)
             wide[c, t, pl.ds(far, 1)] = jnp.zeros((1, cols, 3 * ch), bf16)
 
-    send_count.wait()
-    count_chip[...] = count_own[...] + count_core[...]
-    plane_counts = [
-        push(count_chip, count_plane.at[i], cp_sem.at[0], cp_sem.at[1], peer) for i, peer in enumerate(plane_peers)
-    ]
-
     for copy in load_weight:
         copy.wait()
     load_sums = load(ema_sum_hbm, ema_sum, clips + 5 + taps)
     last = taps - 1
     send_stat2 = []
     for c in range(clips):
-        for a in range(taps):
-            have = frames - (last - a)
-            left = jnp.concatenate(
-                [wide[c, :have, b:b + rows].reshape(have * per_frame, 3 * ch) for b in range(3)], axis=1
-            )
-            right = weight[a].reshape(9 * ch, ch)
-            part = jnp.dot(left, right, preferred_element_type=f32)
-            start = (last - a) * per_frame
-            if a == 0:
-                hid[c, :start] = vid[c].reshape(per_clip, ch)[:start].astype(f32)
-                hid[c, start:] = vid[c].reshape(per_clip, ch)[start:].astype(f32) + part
-            else:
-                hid[c, start:] = hid[c, start:] + part
+        rows_at_once = rows // PIECES
+        for t in range(frames):
+            for r in range(0, rows, rows_at_once):
+                place = pl.ds(t * per_frame + r * cols, rows_at_once * cols)
+                total = vid[c, t, r:r + rows_at_once].reshape(-1, ch).astype(f32)
+                for a in range(taps):
+                    from_frame = t + a - last
+                    if from_frame < 0:
+                        continue
+                    left = jnp.concatenate(
+                        [
+                            wide[c, from_frame, r + b:r + b + rows_at_once].reshape(-1, 3 * ch)
+                            for b in range(3)
+                        ],
+                        axis=1,
+                    )
+                    total = total + jnp.dot(left, weight[a].reshape(9 * ch, ch), preferred_element_type=f32)
+                hid[c, place] = total
 
         def add(i, carry, c=c):
             v = hid[c, ds(i * block, block)]
@@ -253,14 +255,9 @@
         stat2[c, 1:2] = second.sum(axis=0, keepdims=True)
         send_stat2.append(push(stat2.at[c], got2.at[c], part_send.at[2 + c], part_recv.at[2 + c], partner))
 
-    every_count = remote(count_plane, count_plane, cp_sem.at[0], cp_sem.at[1], partner)
-    every_count.wait()
-    total = count_chip[...]
-    for i in range(NEAR):
-        total = total + count_plane[i]
-    count_z[z] = total
-    for peer in z_peers:
-        push(count_z.at[z], count_z.at[z], cz_sem.at[0], cz_sem.at[1], peer)
+    for c in range(1, clips):
+        mark(c)
+    send_count = push(count_own, count_core, cc_sem.at[0], cc_sem.at[1], other_core)
 
     far_half, own_half = ds((1 - core) * HALF, HALF), ds(core * HALF, HALF)
     for c in range(clips):
@@ -281,15 +278,14 @@
                 )
                 raw[i] = part if c == 0 else raw[i] + part
 
-    write_act = load(act2, act_hbm, clips + 6 + taps)
-
     def sums_of(i, w):
         start = ((1 - core) if i == 0 else core) * HALF + w * WAVE
         c = clips - 1
-        mine = raw[i, w * WAVE:(w + 1) * WAVE] + jnp.dot(
-            member[ds(start, WAVE), c * per_clip:(c + 1) * per_clip],
-            act2[c * per_clip:(c + 1) * per_clip], preferred_element_type=f32,
-        )
+        mine = raw[i, w * WAVE:(w + 1) * WAVE]
+        for k in range(c * per_clip, (c + 1) * per_clip, per_clip // 2):
+            mine = mine + jnp.dot(
+                member[ds(start, WAVE), k:k + per_clip // 2], act2[k:k + per_clip // 2], preferred_element_type=f32
+            )
         high = mine.astype(bf16)
         low = (mine - high.astype(f32)).astype(bf16)
         return jnp.dot(high, proj_ref[...], preferred_element_type=f32) + jnp.dot(
@@ -309,6 +305,11 @@
         for i, peer in enumerate(plane_peers):
             push(half.at[w, ds(plane_chunks[i] * CHUNK, CHUNK)], plane_in.at[w, i], rs_send.at[w], rs_recv.at[w], peer)
 
+    send_count.wait()
+    count_chip[...] = count_own[...] + count_core[...]
+    for i, peer in enumerate(plane_peers):
+        push(count_chip, count_plane.at[i], cp_sem.at[0], cp_sem.at[1], peer)
+
     for w in range(WAVES):
         remote(plane_in.at[w], plane_in.at[w], rs_send.at[w], rs_recv.at[w], partner).wait()
         total = raw[1, ds(w * WAVE + own_chunk * CHUNK, CHUNK)]
@@ -335,6 +336,7 @@
                 member[:, at:at + 256], book[...], (((0,), (0,)), ((), ())), preferred_element_type=f32
             )
             value = jnp.dot(act2[at:at + 256], proj_ref[...], preferred_element_type=f32)
+            latent[at:at + 256] = value
             gap = value - (picked[:, :EMB] + picked[:, EMB:])
             part += fold(gap * gap)
         errs[pl.ds(c, 1)] = part.sum(axis=0, keepdims=True)
@@ -342,6 +344,15 @@
     for c in range(clips):
         distances(c)
     send_err = push(errs, got_err, part_send.at[2 + clips], part_recv.at[2 + clips], partner)
+
+    every_count = remote(count_plane, count_plane, cp_sem.at[0], cp_sem.at[1], partner)
+    every_count.wait()
+    total = count_chip[...]
+    for i in range(NEAR):
+        total = total + count_plane[i]
+    count_z[z] = total
+    for peer in z_peers:
+        push(count_z.at[z], count_z.at[z], cz_sem.at[0], cz_sem.at[1], peer)
 
     base = core * HALF
     for w in range(WAVES):
@@ -355,77 +366,45 @@
         for peer in plane_peers:
             push(sums_ref.at[own_rows], sums_ref.at[own_rows], ag_send.at[w], ag_recv.at[w], peer)
 
+    send_err.wait()
+    err = (errs[...] + got_err[...]).sum(axis=1, keepdims=True) / (2 * per_clip * EMB)
+    err_ref[...] = jnp.broadcast_to(err, err_ref.shape)
+
+    forward = []
+    for w in range(WAVES):
+        remote(plane_in.at[w], plane_in.at[w], ag_send.at[w], ag_recv.at[w], partner).wait()
+        here = ds(base + w * WAVE, WAVE)
+        forward.append(push(sums_ref.at[here], sums_ref.at[here], fw_send.at[w], fw_recv.at[w], other_core))
     arrived = count_z.at[pl.ds(0, Z - 1)]
     remote(arrived, arrived, cz_sem.at[0], cz_sem.at[1], partner).wait()
     total = count_z[0]
     for i in range(1, Z):
         total = total + count_z[i]
     counts_ref[...] = total
-    send_err.wait()
-    err = (errs[...] + got_err[...]).sum(axis=1, keepdims=True) / (2 * per_clip * EMB)
-    err_ref[...] = jnp.broadcast_to(err, err_ref.shape)
-
-    forward = []
-    for w in range(WAVES):
-        remote(plane_in.at[w], plane_in.at[w], ag_send.at[w], ag_recv.at[w], partner).wait()
-        here = ds(base + w * WAVE, WAVE)
-        forward.append(push(sums_ref.at[here], sums_ref.at[here], fw_send.at[w], fw_recv.at[w], other_core))
     for copy in forward:
         copy.wait()
-    write_act.wait()
-
-
-def finish(
-    act_hbm, sums_hbm, counts_hbm, ema_sum_hbm, ema_count_hbm, proj_hbm, err_hbm,
-    latent_hbm, book_hbm, count_ref, err_out,
-    act2, sums, counts, ema_sum, ema_count, proj, err, latent, book, in_sem, out_sem,
-):
-    tokens = act2.shape[0]
+
+
+def finish(latent, ema_sum, sums, counts, err, ema_count, latent_hbm, book_hbm, count_ref, err_out, book, out_sem):
     parts = 4
-    step = tokens // parts
     turn = CODES // parts
-
-    def load(src, dst, i):
-        copy = pltpu.make_async_copy(src, dst, in_sem.at[i])
-        copy.start()
-        return copy
-
-    small = [
-        load(src, dst, i)
-        for i, (src, dst) in enumerate(
-            [(proj_hbm, proj), (counts_hbm, counts), (ema_count_hbm, ema_count), (err_hbm, err)]
-        )
-    ]
-    acts = [load(act_hbm.at[pl.ds(i * step, step)], act2.at[pl.ds(i * step, step)], 4 + i) for i in range(parts)]
-    terms = [load(sums_hbm, sums, 4 + parts), load(ema_sum_hbm, ema_sum, 5 + parts)]
-    for copy in small:
-        copy.wait()
-    out = []
-
-    def put(src, dst):
-        copy = pltpu.make_async_copy(src, dst, out_sem.at[len(out)])
-        copy.start()
-        out.append(copy)
-
-    for i in range(parts):
-        acts[i].wait()
-        at = pl.ds(i * step, step)
-        latent[at] = jnp.dot(act2[at], proj[...], preferred_element_type=f32)
-        put(latent.at[at], latent_hbm.at[at])
+    write_latent = pltpu.make_async_copy(latent, latent_hbm, out_sem.at[parts])
+    write_latent.start()
     code_count = DECAY * ema_count[...] + (1.0 - DECAY) * counts[...]
     count_ref[...] = code_count
     smooth = smoothed(code_count)
     for i in range(err_out.shape[0]):
         err_out[i] = err[i, 0]
-    for copy in terms:
-        copy.wait()
+    out = [write_latent]
     for i in range(parts):
         for j in range(i * turn // SPAN, (i + 1) * turn // SPAN):
             at = pl.ds(j * SPAN, SPAN)
             scale = jnp.concatenate([down(smooth[:, j * SPAN:(j + 1) * SPAN])] * (EMB // SPAN), axis=1)
             book[at] = (DECAY * ema_sum[at] + (1.0 - DECAY) * sums[at].astype(f32)) / scale
         at = pl.ds(i * turn, turn)
-        put(book.at[at], book_hbm.at[at])
+        copy = pltpu.make_async_copy(book.at[at], book_hbm.at[at], out_sem.at[i])
+        copy.start()
+        out.append(copy)
     for copy in out:
         copy.wait()
 
@@ -435,7 +414,6 @@
     tokens = clips * frames * rows * cols
     taps = min(frames, conv_weight.shape[0])
     vmem = pl.BlockSpec(memory_space=pltpu.VMEM)
-    near = pl.BlockSpec(memory_space=pl.ANY)
     hbm = pl.BlockSpec(memory_space=pltpu.HBM)
     dma = pltpu.SemaphoreType.DMA
     V = pltpu.VMEM
@@ -443,16 +421,17 @@
     keep = lambda a: pltpu.with_memory_space_constraint(a, pltpu.HBM)
     video, conv_weight, proj_weight, codes, ema_sum, count_row = map(keep, (video, conv_weight, proj_weight, codes, ema_sum, count_row))
     gain_first, gain_second = keep(gain_first.reshape(1,-1)), keep(gain_second.reshape(1,-1))
-    act2, sums, counts, err = pl.pallas_call(
+    latent, terms, sums, counts, err = pl.pallas_call(
         kernel,
         out_shape=(
-            jax.ShapeDtypeStruct((tokens, ch), bf16),
+            jax.ShapeDtypeStruct((tokens, EMB), f32),
+            jax.ShapeDtypeStruct((CODES, EMB), f32),
             jax.ShapeDtypeStruct((CODES, EMB), bf16),
             jax.ShapeDtypeStruct((1, CODES), f32),
             jax.ShapeDtypeStruct((8, 128), f32),
         ),
         in_specs=[hbm] * 8,
-        out_specs=(near, vmem, vmem, vmem),
+        out_specs=(vmem,) * 5,
         scratch_shapes=[
             V(video.shape, bf16),
             V((clips, frames, 1, cols, ch), bf16),
@@ -462,7 +441,6 @@
             V((tokens, ch), bf16),
             V((CODES, tokens), bf16),
             V((CODES, 2 * EMB), bf16),
-            V((CODES, EMB), f32),
             V((2, HALF, EMB), f32),
             V(codes.shape, jnp.int32),
             V((tokens // 128, 128), jnp.int32),
@@ -473,7 +451,7 @@
             V((NEAR, 1, CODES), f32), V((Z, 1, CODES), f32),
             V((WAVES, WAVE, EMB), bf16), V((WAVES, WAVE, EMB), bf16), V((WAVES, WAVE, EMB), bf16),
             V((WAVES, NEAR, CHUNK, EMB), bf16), V((WAVES, Z, CHUNK, EMB), bf16),
-            dma((clips + taps + 7,)),
+            dma((clips + taps + 6,)),
             dma((clips + 3,)), dma((clips + 3,)), dma((2,)),
         ] + [dma((WAVES,))] * 10 + [dma((2,))] * 2,
         compiler_params=pltpu.CompilerParams(
@@ -491,15 +469,13 @@
             jax.ShapeDtypeStruct((1, CODES), f32),
             jax.ShapeDtypeStruct((clips,), f32),
         ),
-        in_specs=[near, near, near, hbm, hbm, hbm, near],
+        in_specs=[vmem] * 6,
         out_specs=(hbm, hbm, vmem, pl.BlockSpec(memory_space=pltpu.SMEM)),
         scratch_shapes=[
-            V((tokens, ch), bf16), V((CODES, EMB), bf16), V((1, CODES), f32), V((CODES, EMB), f32),
-            V((1, CODES), f32), V(proj_weight.shape, bf16), V((8, 128), f32),
-            V((tokens, EMB), f32), V((CODES, EMB), f32), dma((10,)), dma((8,)),
+            V((CODES, EMB), f32), dma((5,)),
         ],
         compiler_params=pltpu.CompilerParams(vmem_limit_bytes=16 << 20),
-    )(act2, sums, counts, ema_sum, count_row, proj_weight, err)
+    )(latent, terms, sums, counts, err, count_row)
     return (latent.reshape(video.shape[:4] + (EMB,)), codebook, code_count.reshape(-1), clip_error)
 
 

time: 50 us -> 45.9 us (0.918)
  Pallas kernels: 49.3 us -> 45.1 us
    pallas_call x1, Pallas kernels: 45.3 us -> 42.2 us  [body(): pl.pallas_call(kernel, out_shape=(jax.ShapeDtypeStruct((tokens, EMB), f32...]
    pallas_call x1, Pallas kernels: 3.95 us -> 2.99 us  [body(): pl.pallas_call(finish, out_shape=(jax.ShapeDtypeStruct((tokens, EMB), f32...]
where the time goes in v3:
time: 45.9 us; the launch traced here: 45.8 us
  Pallas kernels  45.1 us (98%)
  between operations  0.64 us (1%)
    pallas_call x1, Pallas kernels, body(): pl.pallas_call(kernel, out_shape=(jax.ShapeDtypeStruct((tokens, EMB), f32...  42.2 us
    pallas_call x1, Pallas kernels, body(): pl.pallas_call(finish, out_shape=(jax.ShapeDtypeStruct((tokens, EMB), f32...  2.99 us

profile of v3, /device:TPU:1, one launch (start us, length us, event | category | flops | bytes accessed | tf_op | source)
XLA Modules:
  0.0 45.8 jit_solution(17330392801432678774)
XLA Ops:
  0.6 42.2 %shard_map.111 = (f32[2048,256]{1,0:T(8,128)S(1)}, f32[1024,256]{1,0:T(8,128)S(1)}, bf16[1024,256]{1,0:T(8,128)(2,1)S(1)}, f32[1,1024]{1,0:T(1,128)S(1)}, f32[8,128]{1,0:T(8,128)S(1)}) custom-call(bf16[2,2,16,32,256]{4,3,2,1,0:T(8,128)(2,1)} %video_hbm.1, bf16[3,3,3,256,256]{4,3,2,1,0:T(8,128)(2,1)} %weight_hbm.1, f32[1,256]{1,0:T(1,128)} %bitcast.7, ...), custom_call_target="tpu_custom_call" | custom-call | tf_op jit(solution)/shard_map/pallas_call | solution.py:424
  42.8 3.0 %shard_map.112 = (f32[2048,256]{1,0:T(8,128)}, f32[1024,256]{1,0:T(8,128)}, f32[1,1024]{1,0:T(1,128)}, f32[2]{0:T(128)}) custom-call(f32[2048,256]{1,0:T(8,128)S(1)} %get-tuple-element.13.latent, f32[1024,256]{1,0:T(8,128)S(1)} %get-tuple-element.14.ema_sum, bf16[1024,256]{1,0:T(8,128)(2,1)S(1)} %get-tuple-element.15.sums, ...), custom_call_target="tpu_custom_call" | custom-call | tf_op jit(solution)/shard_map/pallas_call | solution.py:464

commit v4 on v3

--- a/solution.py
+++ b/solution.py
@@ -21,6 +21,7 @@
 CHUNK = WAVE // PLANE
 NEAR = PLANE - 1
 SPAN = 128
+CORE_PIECES = 1
 PIECES = 2
 bf16, f32 = jnp.bfloat16, jnp.float32
 
@@ -99,11 +100,14 @@
     other_core = address(x, y, z, 1 - core)
     plane_peers = [address((x + dx) % X, (y + dy) % Y, z, core) for dx, dy in steps]
     plane_chunks = [(y + dy) % Y * X + (x + dx) % X for dx, dy in steps]
+    from_chunks = [(y - dy + Y) % Y * X + (x - dx + X) % X for dx, dy in steps]
     own_chunk = y * X + x
     z_peers = [address(x, y, (z + d) % Z, core) for d in z_steps]
 
     barrier = pltpu.get_barrier_semaphore()
-    everyone = plane_peers + z_peers + [other_core]
+    direct = [i for i, (dx, dy) in enumerate(steps) if min(dx, X - dx) + min(dy, Y - dy) <= 1]
+    cross = {i: address((x + steps[i][0]) % X, (y + steps[i][1]) % Y, z, 1 - core) for i in direct}
+    everyone = plane_peers + z_peers + [other_core] + list(cross.values())
     for peer in everyone:
         pl.semaphore_signal(barrier, inc=1, device_id=peer, device_id_type=MESH)
 
@@ -145,24 +149,20 @@
             codes_at[pl.ds((c * frames + t) * quads, quads)] = jnp.concatenate(
                 [codes_in[c, t, pl.ds(p, quads, stride=lines)] for p in range(lines)], axis=1
             )
-    def mark(c):
-        first, end = c * frames * quads, (c + 1) * frames * quads
-
-        def some(i, carry):
-            k = pl.multiple_of(i * SPAN, SPAN)
-            number = lax.broadcasted_iota(jnp.int32, (SPAN, block), 0) + k
-            total = jnp.zeros((SPAN, block), f32)
-            for j in range(first, end):
-                hit = jnp.where(number == codes_at[j:j + 1], 1.0, 0.0)
-                total += hit
-                member[pl.ds(k, SPAN), j * block:(j + 1) * block] = hit.astype(bf16)
-            found = jnp.broadcast_to(total.sum(axis=1, keepdims=True), (SPAN, SPAN)).T[:1]
-            count_own[:, pl.ds(k, SPAN)] = found if c == 0 else count_own[:, pl.ds(k, SPAN)] + found
-            return carry
-
-        lax.fori_loop(0, CODES // SPAN, some, 0)
-
-    mark(0)
+    def mark(i, carry):
+        k = pl.multiple_of(i * SPAN, SPAN)
+        number = (lax.broadcasted_iota(jnp.int32, (SPAN, block), 0) + k).astype(jnp.int16)
+        total = jnp.zeros((SPAN, block), bf16)
+        for j in range(clips * frames * quads):
+            hit = jnp.where(number == codes_at[j:j + 1].astype(jnp.int16), jnp.ones((), bf16), jnp.zeros((), bf16))
+            total += hit
+            member[pl.ds(k, SPAN), j * block:(j + 1) * block] = hit
+        found = total.astype(f32).sum(axis=1, keepdims=True)
+        count_own[:, pl.ds(k, SPAN)] = jnp.broadcast_to(found, (SPAN, SPAN)).T[:1]
+        return carry
+
+    lax.fori_loop(0, CODES // SPAN, mark, 0)
+    send_count = push(count_own, count_core, cc_sem.at[0], cc_sem.at[1], other_core)
 
     members = per_clip * 2 * (ch // GROUPS)
     group = ch // GROUPS
@@ -255,9 +255,10 @@
         stat2[c, 1:2] = second.sum(axis=0, keepdims=True)
         send_stat2.append(push(stat2.at[c], got2.at[c], part_send.at[2 + c], part_recv.at[2 + c], partner))
 
-    for c in range(1, clips):
-        mark(c)
-    send_count = push(count_own, count_core, cc_sem.at[0], cc_sem.at[1], other_core)
+    send_count.wait()
+    count_chip[...] = count_own[...] + count_core[...]
+    for i, peer in enumerate(plane_peers):
+        push(count_chip, count_plane.at[i], cp_sem.at[0], cp_sem.at[1], peer)
 
     far_half, own_half = ds((1 - core) * HALF, HALF), ds(core * HALF, HALF)
     for c in range(clips):
@@ -286,29 +287,31 @@
             mine = mine + jnp.dot(
                 member[ds(start, WAVE), k:k + per_clip // 2], act2[k:k + per_clip // 2], preferred_element_type=f32
             )
-        high = mine.astype(bf16)
-        low = (mine - high.astype(f32)).astype(bf16)
+        return mine
+
+    def projected(v):
+        high = v.astype(bf16)
+        low = (v - high.astype(f32)).astype(bf16)
         return jnp.dot(high, proj_ref[...], preferred_element_type=f32) + jnp.dot(
             low, proj_ref[...], preferred_element_type=f32
         )
 
     send_core = []
-    for w in range(WAVES):
-        core_out[w] = sums_of(0, w).astype(bf16)
-        send_core.append(push(core_out.at[w], core_in.at[w], core_send.at[w], core_recv.at[w], other_core))
-    for w in range(WAVES):
-        own = sums_of(1, w)
-        send_core[w].wait()
-        own = own + core_in[w].astype(f32)
-        raw[1, w * WAVE:(w + 1) * WAVE] = own
-        half[w] = own.astype(bf16)
+    outgoing = [sums_of(0, w).astype(bf16) for w in range(WAVES)]
+    for w in range(WAVES):
+        core_out[w] = outgoing[w]
+    for w in range(WAVES):
+        for p in range(CORE_PIECES):
+            at = pl.ds(p * (WAVE // CORE_PIECES), WAVE // CORE_PIECES)
+            push(core_out.at[w, at], core_in.at[w, at], core_send.at[w], core_recv.at[w], other_core)
+    own = [sums_of(1, w) for w in range(WAVES)]
+    for w in range(WAVES):
+        remote(core_out.at[w], core_in.at[w], core_send.at[w], core_recv.at[w], other_core).wait()
+        both = own[w] + core_in[w].astype(f32)
+        raw[1, w * WAVE:(w + 1) * WAVE] = both
+        half[w] = both.astype(bf16)
         for i, peer in enumerate(plane_peers):
             push(half.at[w, ds(plane_chunks[i] * CHUNK, CHUNK)], plane_in.at[w, i], rs_send.at[w], rs_recv.at[w], peer)
-
-    send_count.wait()
-    count_chip[...] = count_own[...] + count_core[...]
-    for i, peer in enumerate(plane_peers):
-        push(count_chip, count_plane.at[i], cp_sem.at[0], cp_sem.at[1], peer)
 
     for w in range(WAVES):
         remote(plane_in.at[w], plane_in.at[w], rs_send.at[w], rs_recv.at[w], partner).wait()
@@ -318,6 +321,15 @@
         z_buf[w, z] = total.astype(bf16)
         for peer in z_peers:
             push(z_buf.at[w, z], z_buf.at[w, z], z_send.at[w], z_recv.at[w], peer)
+
+    every_count = remote(count_plane, count_plane, cp_sem.at[0], cp_sem.at[1], partner)
+    every_count.wait()
+    total = count_chip[...]
+    for i in range(NEAR):
+        total = total + count_plane[i]
+    count_z[z] = total
+    for peer in z_peers:
+        push(count_z.at[z], count_z.at[z], cz_sem.at[0], cz_sem.at[1], peer)
 
     load_sums.wait()
     smooth = smoothed(ema_count_ref[...])
@@ -345,15 +357,6 @@
         distances(c)
     send_err = push(errs, got_err, part_send.at[2 + clips], part_recv.at[2 + clips], partner)
 
-    every_count = remote(count_plane, count_plane, cp_sem.at[0], cp_sem.at[1], partner)
-    every_count.wait()
-    total = count_chip[...]
-    for i in range(NEAR):
-        total = total + count_plane[i]
-    count_z[z] = total
-    for peer in z_peers:
-        push(count_z.at[z], count_z.at[z], cz_sem.at[0], cz_sem.at[1], peer)
-
     base = core * HALF
     for w in range(WAVES):
         arrived = z_buf.at[w, pl.ds(0, Z - 1)]
@@ -362,27 +365,33 @@
         for i in range(1, Z):
             total = total + z_buf[w, i].astype(f32)
         own_rows = ds(base + w * WAVE + own_chunk * CHUNK, CHUNK)
-        sums_ref[own_rows] = total.astype(bf16)
-        for peer in plane_peers:
-            push(sums_ref.at[own_rows], sums_ref.at[own_rows], ag_send.at[w], ag_recv.at[w], peer)
+        sums_ref[own_rows] = projected(total).astype(bf16)
+        for i, peer in enumerate(plane_peers):
+            push(sums_ref.at[own_rows], sums_ref.at[own_rows], ag_send.at[w], ag_recv.at[w, i], peer)
+            if i in cross:
+                push(sums_ref.at[own_rows], sums_ref.at[own_rows], fw_send.at[w], fw_recv.at[w], cross[i])
+        push(sums_ref.at[own_rows], sums_ref.at[own_rows], fw_send.at[w], fw_recv.at[w], other_core)
 
     send_err.wait()
     err = (errs[...] + got_err[...]).sum(axis=1, keepdims=True) / (2 * per_clip * EMB)
     err_ref[...] = jnp.broadcast_to(err, err_ref.shape)
 
-    forward = []
-    for w in range(WAVES):
-        remote(plane_in.at[w], plane_in.at[w], ag_send.at[w], ag_recv.at[w], partner).wait()
-        here = ds(base + w * WAVE, WAVE)
-        forward.append(push(sums_ref.at[here], sums_ref.at[here], fw_send.at[w], fw_recv.at[w], other_core))
+    for w in range(WAVES):
+        for i in sorted(range(NEAR), key=lambda i: (i in cross, -i)):
+            here = sums_ref.at[ds(base + w * WAVE + from_chunks[i] * CHUNK, CHUNK)]
+            remote(here, here, ag_send.at[w], ag_recv.at[w, i], partner).wait_recv()
+            if i not in cross:
+                push(here, here, fw_send.at[w], fw_recv.at[w], other_core)
     arrived = count_z.at[pl.ds(0, Z - 1)]
     remote(arrived, arrived, cz_sem.at[0], cz_sem.at[1], partner).wait()
     total = count_z[0]
     for i in range(1, Z):
         total = total + count_z[i]
     counts_ref[...] = total
-    for copy in forward:
-        copy.wait()
+    for w in range(WAVES):
+        remote(plane_in.at[w], plane_in.at[w], ag_send.at[w], fw_recv.at[w], partner).wait_send()
+        mine = sums_ref.at[ds(base + w * WAVE, WAVE)]
+        remote(mine, mine, fw_send.at[w], fw_recv.at[w], other_core).wait()
 
 
 def finish(latent, ema_sum, sums, counts, err, ema_count, latent_hbm, book_hbm, count_ref, err_out, book, out_sem):
@@ -453,7 +462,7 @@
             V((WAVES, NEAR, CHUNK, EMB), bf16), V((WAVES, Z, CHUNK, EMB), bf16),
             dma((clips + taps + 6,)),
             dma((clips + 3,)), dma((clips + 3,)), dma((2,)),
-        ] + [dma((WAVES,))] * 10 + [dma((2,))] * 2,
+        ] + [dma((WAVES,))] * 7 + [dma((WAVES, NEAR))] + [dma((WAVES,))] * 2 + [dma((2,))] * 2,
         compiler_params=pltpu.CompilerParams(
             collective_id=0, has_side_effects=True, vmem_limit_bytes=32 << 20
         ),

time: 45.9 us -> 45.7 us (level)
  no operation moved by 1% of the time
where the time goes in v4:
time: 45.7 us; the launch traced here: 45.6 us
  Pallas kernels  44.9 us (98%)
  between operations  0.64 us (1%)
    pallas_call x1, Pallas kernels, body(): pl.pallas_call(kernel, out_shape=(jax.ShapeDtypeStruct((tokens, EMB), f32...  42 us
    pallas_call x1, Pallas kernels, body(): pl.pallas_call(finish, out_shape=(jax.ShapeDtypeStruct((tokens, EMB), f32...  2.99 us

profile of v4, /device:TPU:1, one launch (start us, length us, event | category | flops | bytes accessed | tf_op | source)
XLA Modules:
  0.0 45.6 jit_solution(15755516316403661791)
XLA Ops:
  0.6 42.0 %shard_map.111 = (f32[2048,256]{1,0:T(8,128)S(1)}, f32[1024,256]{1,0:T(8,128)S(1)}, bf16[1024,256]{1,0:T(8,128)(2,1)S(1)}, f32[1,1024]{1,0:T(1,128)S(1)}, f32[8,128]{1,0:T(8,128)S(1)}) custom-call(bf16[2,2,16,32,256]{4,3,2,1,0:T(8,128)(2,1)} %video_hbm.1, bf16[3,3,3,256,256]{4,3,2,1,0:T(8,128)(2,1)} %weight_hbm.1, f32[1,256]{1,0:T(1,128)} %bitcast.7, ...), custom_call_target="tpu_custom_call" | custom-call | tf_op jit(solution)/shard_map/pallas_call | solution.py:433
  42.6 3.0 %shard_map.112 = (f32[2048,256]{1,0:T(8,128)}, f32[1024,256]{1,0:T(8,128)}, f32[1,1024]{1,0:T(1,128)}, f32[2]{0:T(128)}) custom-call(f32[2048,256]{1,0:T(8,128)S(1)} %get-tuple-element.13.latent, f32[1024,256]{1,0:T(8,128)S(1)} %get-tuple-element.14.ema_sum, bf16[1024,256]{1,0:T(8,128)(2,1)S(1)} %get-tuple-element.15.sums, ...), custom_call_target="tpu_custom_call" | custom-call | tf_op jit(solution)/shard_map/pallas_call | solution.py:473

commit v5 on v4

--- a/solution.py
+++ b/solution.py
@@ -21,8 +21,7 @@
 CHUNK = WAVE // PLANE
 NEAR = PLANE - 1
 SPAN = 128
-CORE_PIECES = 1
-PIECES = 2
+PIECES = 4
 bf16, f32 = jnp.bfloat16, jnp.float32
 
 
@@ -297,13 +296,9 @@
         )
 
     send_core = []
-    outgoing = [sums_of(0, w).astype(bf16) for w in range(WAVES)]
-    for w in range(WAVES):
-        core_out[w] = outgoing[w]
-    for w in range(WAVES):
-        for p in range(CORE_PIECES):
-            at = pl.ds(p * (WAVE // CORE_PIECES), WAVE // CORE_PIECES)
-            push(core_out.at[w, at], core_in.at[w, at], core_send.at[w], core_recv.at[w], other_core)
+    for w in range(WAVES):
+        core_out[w] = sums_of(0, w).astype(bf16)
+        push(core_out.at[w], core_in.at[w], core_send.at[w], core_recv.at[w], other_core)
     own = [sums_of(1, w) for w in range(WAVES)]
     for w in range(WAVES):
         remote(core_out.at[w], core_in.at[w], core_send.at[w], core_recv.at[w], other_core).wait()

time: 45.7 us -> 45.9 us (level)
  no operation moved by 1% of the time
where the time goes in v5:
time: 45.9 us; the launch traced here: 45.8 us
  Pallas kernels  45.1 us (98%)
  between operations  0.64 us (1%)
    pallas_call x1, Pallas kernels, body(): pl.pallas_call(kernel, out_shape=(jax.ShapeDtypeStruct((tokens, EMB), f32...  42.1 us
    pallas_call x1, Pallas kernels, body(): pl.pallas_call(finish, out_shape=(jax.ShapeDtypeStruct((tokens, EMB), f32...  2.99 us

profile of v5, /device:TPU:1, one launch (start us, length us, event | category | flops | bytes accessed | tf_op | source)
XLA Modules:
  0.0 45.8 jit_solution(14308169938130795728)
XLA Ops:
  0.6 42.1 %shard_map.111 = (f32[2048,256]{1,0:T(8,128)S(1)}, f32[1024,256]{1,0:T(8,128)S(1)}, bf16[1024,256]{1,0:T(8,128)(2,1)S(1)}, f32[1,1024]{1,0:T(1,128)S(1)}, f32[8,128]{1,0:T(8,128)S(1)}) custom-call(bf16[2,2,16,32,256]{4,3,2,1,0:T(8,128)(2,1)} %video_hbm.1, bf16[3,3,3,256,256]{4,3,2,1,0:T(8,128)(2,1)} %weight_hbm.1, f32[1,256]{1,0:T(1,128)} %bitcast.7, ...), custom_call_target="tpu_custom_call" | custom-call | tf_op jit(solution)/shard_map/pallas_call | solution.py:428
  42.8 3.0 %shard_map.112 = (f32[2048,256]{1,0:T(8,128)}, f32[1024,256]{1,0:T(8,128)}, f32[1,1024]{1,0:T(1,128)}, f32[2]{0:T(128)}) custom-call(f32[2048,256]{1,0:T(8,128)S(1)} %get-tuple-element.13.latent, f32[1024,256]{1,0:T(8,128)S(1)} %get-tuple-element.14.ema_sum, bf16[1024,256]{1,0:T(8,128)(2,1)S(1)} %get-tuple-element.15.sums, ...), custom_call_target="tpu_custom_call" | custom-call | tf_op jit(solution)/shard_map/pallas_call | solution.py:468
